TPU v7x, 512 devices: a whole 4x4x16 slice. The times are simulated.
512 devices in a mesh: dp: 64 (over x, y, z_hi), tensor: 8 (over z_lo, core).
Axes of the slice: x: 4, y: 4, z: 16 (z_hi: 4, z_lo: 4; z = z_hi * 4 + z_lo), core: 2. Of those that a mesh axis runs over, the one named last changes fastest.
Arguments:
- master: float32 [3, 8, 1024, 2048], P(None, None, 'dp', 'tensor'), may hold values from -6 to 6
- moment_one: float32 [3, 8, 1024, 2048], P(None, None, 'dp', 'tensor'), may hold values from -4 to 4
- moment_two: float32 [3, 8, 1024, 2048], P(None, None, 'dp', 'tensor'), may hold values from 0.01 to 1
- gradients: bfloat16 [3, 8, 1024, 2048], P(None, None, 'dp', 'tensor'), may hold values from -10000 to 10000
- norm_gain: float32 [2048], replicated, may hold values from 0.1 to 1.9
- hidden_in: bfloat16 [4, 2048, 2048], P(None, ('dp', 'tensor')), may hold values from -6 to 6
- expert_ids: int32 [4, 2048, 2], P(None, ('dp', 'tensor')), may hold values from 0 to 7, all different within a row; in each aligned block of 4 rows (0 to 3, 4 to 7, ..., all dimensions but the last counted through in order) at most 2 rows name the same one
- route_weights: float32 [4, 2048, 2], P(None, ('dp', 'tensor')), may hold values from 0.05 to 1
Outputs:
- new_master: float32 [3, 8, 1024, 2048], P(None, None, 'dp', 'tensor')
- new_moment_one: float32 [3, 8, 1024, 2048], P(None, None, 'dp', 'tensor')
- new_moment_two: float32 [3, 8, 1024, 2048], P(None, None, 'dp', 'tensor')
- served_weights: bfloat16 [3, 8192, 2048], P(None, 'dp')
- decoded: bfloat16 [4, 2048, 2048], P(None, ('dp', 'tensor'))
Inputs may be any that keep to these rules, and one draw needn't show every extreme that they name: `expert_ids`: A row names 2 different experts; in each step the 4 rows of one device name one expert at most 2 times.
All inputs are finite; a program needn't handle non-finite values.
Results may differ from a plain program's by a relative error of at most 0.0067.
Values may be sent and summed in bfloat16 or wider, within the bound.
A program may use at most 64 MiB of HBM per device.

v0:
```python
from functools import partial
import math

import jax
import jax.numpy as jnp
from jax import lax
from jax.sharding import Mesh
from jax.sharding import PartitionSpec as P

DP = ("dp_0", "dp_1", "dp_2")
TENSOR = ("tensor_0", "tensor_1")
DP_TENSOR = ("dp_0", "dp_1", "dp_2", "tensor_0", "tensor_1")


beta_one = 0.9
beta_two = 0.95
learn_rate = 0.02
decay_rate = 0.1
adam_eps = 1e-08
step_count = 10
norm_eps = 1e-06


def by_axis(array, axes):
    for axis in axes:
        array = lax.psum(array, axis)
    return array


def laid_out(pieces, dim):
    shape = list(pieces.shape[1:])
    shape[dim] *= pieces.shape[0]
    return jnp.moveaxis(pieces, 0, dim).reshape(shape)


def stacked_from(array, axes, turns):
    pieces = array
    for k in turns:
        pieces = lax.all_gather(pieces, axes[k])
    done = turns[::-1]
    back = [done.index(k) for k in range(len(axes))]
    pieces = pieces.transpose(*back, *range(len(axes), pieces.ndim))
    return pieces.reshape(-1, *array.shape)


def gather_axes(array, axes, turns, dim):
    return laid_out(stacked_from(array, axes, turns), dim)


def adam_update(master, moment_one, moment_two, gradients, clip_factor):
    scaled = gradients.astype(jnp.float32) * clip_factor
    first_moment = beta_one * moment_one + (1.0 - beta_one) * scaled
    second = beta_two * moment_two + (1.0 - beta_two) * scaled * scaled
    first_fix = 1.0 - beta_one**step_count
    second_fix = 1.0 - beta_two**step_count
    update = first_moment / first_fix / (jnp.sqrt(second / second_fix) + adam_eps)
    return (master - learn_rate * (update + decay_rate * master), first_moment, second)


def normalize(token_rows, norm_gain):
    widened = token_rows.astype(jnp.float32)
    factor = lax.rsqrt(jnp.mean(widened * widened, axis=1, keepdims=True) + norm_eps)
    return (widened, (widened * factor * norm_gain).astype(jnp.bfloat16))


def route_tables(step_ids, step_gates, expert_count, capacity):
    row_count = step_ids.shape[0]
    top_count = step_ids.shape[1]
    pair_ids = step_ids.reshape(-1)
    shares = (step_gates / jnp.sum(step_gates, axis=1, keepdims=True)).reshape(-1)
    expert_hot = (pair_ids[:, None] == jnp.arange(expert_count, dtype=jnp.int32)[None, :]).astype(
        jnp.int32
    )
    earlier = jnp.cumsum(expert_hot, axis=0) - expert_hot
    slot_index = jnp.sum(earlier * expert_hot, axis=1)
    columns = pair_ids * capacity + slot_index
    pair_slot = (
        columns[:, None] == jnp.arange(expert_count * capacity, dtype=jnp.int32)[None, :]
    ).astype(jnp.float32)
    pair_index = jnp.arange(row_count * top_count, dtype=jnp.int32) // top_count
    pair_row = (pair_index[:, None] == jnp.arange(row_count, dtype=jnp.int32)[None, :]).astype(
        jnp.float32
    )
    combine = jnp.dot(pair_row.T, pair_slot * shares[:, None], precision=lax.Precision.HIGHEST)
    return (pair_slot, pair_row, combine)


def expert_part(received, gate_up, down_rows, hidden_total):
    member_count = received.shape[0]
    slot_count = received.shape[1]
    model_width = received.shape[2]
    flattened = received.reshape(member_count * slot_count, model_width)
    projected = lax.dot_general(
        flattened, gate_up, (((1,), (1,)), ((), ())), preferred_element_type=jnp.float32
    ) / math.sqrt(model_width)
    unit_count = gate_up.shape[0] // 2
    active = (jax.nn.silu(projected[:, :unit_count]) * projected[:, unit_count:]).astype(
        jnp.bfloat16
    )
    partial_out = (
        jnp.dot(active, down_rows, preferred_element_type=jnp.float32) / math.sqrt(hidden_total)
    ).astype(jnp.bfloat16)
    return lax.all_to_all(
        partial_out.reshape(member_count, slot_count, model_width),
        DP,
        split_axis=0,
        concat_axis=0,
        tiled=True,
    )


def per_device(
    master, moment_one, moment_two, gradients, norm_gain, hidden_in, expert_ids, route_weights
):
    widened = gradients.astype(jnp.float32)
    slice_count = lax.axis_size(TENSOR)
    member_count = lax.axis_size(DP)
    expert_count = master.shape[1]
    local_units = master.shape[2]
    local_width = master.shape[3]
    hidden_total = local_units * member_count
    model_width = local_width * slice_count
    entries = 3 * expert_count * hidden_total * model_width
    squares = by_axis(jnp.sum(widened * widened), DP_TENSOR)
    clip_factor = jnp.minimum(1.0, lax.rsqrt(squares / entries + norm_eps))
    new_master, new_one, new_two = adam_update(
        master, moment_one, moment_two, gradients, clip_factor
    )
    rounded = new_master.astype(jnp.bfloat16)
    group_size = member_count // expert_count
    strip_width = local_units // group_size
    device_units = strip_width * member_count
    pieces = rounded.reshape(3, expert_count * group_size, strip_width, local_width)
    strips = lax.all_to_all(pieces, DP, split_axis=1, concat_axis=2, tiled=True)
    owned = gather_axes(strips, TENSOR, (0, 1), 3)
    served = owned.reshape(3, device_units, model_width)
    gate_up = served[:2].reshape(2 * device_units, model_width)
    down_rows = served[2]
    row_count = hidden_in.shape[1]
    top_count = expert_ids.shape[2]
    capacity = min(row_count, max(2, 2 * row_count * top_count // expert_count))
    outputs = []
    for step_index in range(hidden_in.shape[0]):
        widened_rows, normed = normalize(hidden_in[step_index], norm_gain)
        pair_slot, pair_row, combine = route_tables(
            expert_ids[step_index], route_weights[step_index], expert_count, capacity
        )
        select = jnp.dot(pair_slot.T, pair_row, precision=lax.Precision.HIGHEST).astype(
            jnp.bfloat16
        )
        slot_rows = jnp.dot(select, normed, preferred_element_type=jnp.float32).astype(jnp.bfloat16)
        copies = jnp.broadcast_to(
            slot_rows.reshape(expert_count, 1, capacity, model_width),
            (expert_count, group_size, capacity, model_width),
        ).reshape(member_count, capacity, model_width)
        worker = partial(
            expert_part, gate_up=gate_up, down_rows=down_rows, hidden_total=hidden_total
        )
        returned = worker(lax.all_to_all(copies, DP, split_axis=0, concat_axis=0, tiled=True))
        summed = jnp.sum(
            returned.reshape(expert_count, group_size, capacity, model_width).astype(jnp.float32),
            axis=1,
        )
        summed = summed.reshape(expert_count * capacity, model_width)
        result = widened_rows + jnp.dot(combine, summed, precision=lax.Precision.HIGHEST)
        outputs.append(result.astype(jnp.bfloat16))
    return (new_master, new_one, new_two, served, jnp.stack(outputs))


def solution(mesh):
    split = Mesh(
        mesh.devices.reshape(4, 4, 4, 4, 2), ("dp_0", "dp_1", "dp_2", "tensor_0", "tensor_1")
    )
    in_specs = (
        P(None, None, DP, TENSOR),
        P(None, None, DP, TENSOR),
        P(None, None, DP, TENSOR),
        P(None, None, DP, TENSOR),
        P(),
        P(None, DP_TENSOR, None),
        P(None, DP_TENSOR, None),
        P(None, DP_TENSOR, None),
    )
    out_specs = (
        P(None, None, DP, TENSOR),
        P(None, None, DP, TENSOR),
        P(None, None, DP, TENSOR),
        P(None, DP, None),
        P(None, DP_TENSOR, None),
    )
    return jax.shard_map(
        per_device, mesh=split, in_specs=in_specs, out_specs=out_specs, check_vma=False
    )
```

profile of v0, /device:TPU:2, one launch (start us, length us, event | category | flops | bytes accessed | tf_op | source)
XLA Modules:
  0.0 416.8 jit_solution(6039524647803078337)
XLA Ops:
  7.2 1.6 fusion.14
  8.8 14.2 %psum.35 = f32[]{:T(128)} all-reduce(f32[]{:T(128)} %fusion.14), channel_id=1, replica_groups=mesh['dp_0'=4,'dp_1'=4,'dp_2'=4,'tensor_0'=4,'tensor_1'=2] {'dp_0'}, use_global_device_ids=true, to_apply=%region_1.0 | all-reduce | flops 1 | bytes 8 | tf_op jit(solution)/shard_map/psum | solution.py:26
  23.0 8.3 %psum.36 = f32[]{:T(128)} all-reduce(f32[]{:T(128)} %psum.35), channel_id=1, replica_groups=mesh['dp_0'=4,'dp_1'=4,'dp_2'=4,'tensor_0'=4,'tensor_1'=2] {'dp_1'}, use_global_device_ids=true, to_apply=%region_2.0 | all-reduce | flops 1 | bytes 8 | tf_op jit(solution)/shard_map/psum | solution.py:26
  31.4 19.9 %psum.37 = f32[]{:T(128)} all-reduce(f32[]{:T(128)} %psum.36), channel_id=1, replica_groups=mesh['dp_0'=4,'dp_1'=4,'dp_2'=4,'tensor_0'=4,'tensor_1'=2] {'dp_2'}, use_global_device_ids=true, to_apply=%region_3.0 | all-reduce | flops 1 | bytes 8 | tf_op jit(solution)/shard_map/psum | solution.py:26
  51.2 10.9 %psum.38 = f32[]{:T(128)} all-reduce(f32[]{:T(128)} %psum.37), channel_id=1, replica_groups=mesh['dp_0'=4,'dp_1'=4,'dp_2'=4,'tensor_0'=4,'tensor_1'=2] {'tensor_0'}, use_global_device_ids=true, to_apply=%region_4.0 | all-reduce | flops 1 | bytes 8 | tf_op jit(solution)/shard_map/psum | solution.py:26
  62.1 3.1 psum.39
  65.9 2.6 fusion.104
  69.4 10.2 %all-to-all-start = ((bf16[3,64,2,256]{3,2,0,1:T(2,128)(2,1)}), bf16[3,64,2,256]{3,2,0,1:T(2,128)(2,1)S(1)}, u32[]{:S(2)}, u32[]{:S(2)}) async-start(bf16[3,64,2,256]{3,2,0,1:T(2,128)(2,1)} %copy.80), calls=%async_computation | async-start | bytes 393216 | tf_op jit(solution)/shard_map/all_to_all | solution.py:134
  80.9 18.3 %all-to-all-done = bf16[3,64,2,256]{3,2,0,1:T(2,128)(2,1)S(1)} async-done(((bf16[3,64,2,256]{3,2,0,1:T(2,128)(2,1)}), bf16[3,64,2,256]{3,2,0,1:T(2,128)(2,1)S(1)}, u32[]{:S(2)}, u32[]{:S(2)}) %all-to-all-start) | async-done | bytes 196640 | tf_op jit(solution)/shard_map/all_to_all | solution.py:134
  100.3 6.3 %all-to-all-start.7 = ((bf16[64,2,2048]{2,1,0:T(2,128)(2,1)}), bf16[64,2,2048]{2,1,0:T(2,128)(2,1)S(1)}, u32[]{:S(2)}, u32[]{:S(2)}) async-start(bf16[64,2,2048]{2,1,0:T(2,128)(2,1)} %bitcast.25), calls=%async_computation.7 | async-start | bytes 1048576 | tf_op jit(solution)/shard_map/all_to_all | solution.py:159
  107.7 29.2 %all-to-all-done.7 = bf16[64,2,2048]{2,1,0:T(2,128)(2,1)S(1)} async-done(((bf16[64,2,2048]{2,1,0:T(2,128)(2,1)}), bf16[64,2,2048]{2,1,0:T(2,128)(2,1)S(1)}, u32[]{:S(2)}, u32[]{:S(2)}) %all-to-all-start.7) | async-done | bytes 524320 | tf_op jit(solution)/shard_map/all_to_all | solution.py:159
  138.0 10.6 %all-to-all-start.3 = ((bf16[64,2,2048]{2,1,0:T(2,128)(2,1)}), bf16[64,2,2048]{2,1,0:T(2,128)(2,1)S(1)}, u32[]{:S(2)}, u32[]{:S(2)}) async-start(bf16[64,2,2048]{2,1,0:T(2,128)(2,1)} %bitcast.15), calls=%async_computation.3 | async-start | bytes 1048576 | tf_op jit(solution)/shard_map/all_to_all | solution.py:159
  149.7 25.4 %all-to-all-done.3 = bf16[64,2,2048]{2,1,0:T(2,128)(2,1)S(1)} async-done(((bf16[64,2,2048]{2,1,0:T(2,128)(2,1)}), bf16[64,2,2048]{2,1,0:T(2,128)(2,1)S(1)}, u32[]{:S(2)}, u32[]{:S(2)}) %all-to-all-start.3) | async-done | bytes 524320 | tf_op jit(solution)/shard_map/all_to_all | solution.py:159
  176.2 9.1 %all-to-all-start.1 = ((bf16[64,2,2048]{2,1,0:T(2,128)(2,1)}), bf16[64,2,2048]{2,1,0:T(2,128)(2,1)S(1)}, u32[]{:S(2)}, u32[]{:S(2)}) async-start(bf16[64,2,2048]{2,1,0:T(2,128)(2,1)} %bitcast.8), calls=%async_computation.1 | async-start | bytes 1048576 | tf_op jit(solution)/shard_map/all_to_all | solution.py:159
  186.3 32.2 %all_gather.13 = bf16[4,3,1,128,256]{4,3,2,1,0:T(8,128)(2,1)} all-gather(bf16[1,3,1,128,256]{4,3,2,1,0:T(8,128)(2,1)S(1)} %bitcast.109), channel_id=1, replica_groups=mesh['dp_0'=4,'dp_1'=4,'dp_2'=4,'tensor_0'=4,'tensor_1'=2] {'tensor_0'}, dimensions={0}, use_global_device_ids=true | all-gather | bytes 983040 | tf_op jit(solution)/shard_map/all_gather | solution.py:39
  219.9 15.3 %all-to-all-start.5 = ((bf16[64,2,2048]{2,1,0:T(2,128)(2,1)}), bf16[64,2,2048]{2,1,0:T(2,128)(2,1)}, u32[]{:S(2)}, u32[]{:S(2)}) async-start(bf16[64,2,2048]{2,1,0:T(2,128)(2,1)} %bitcast.20), calls=%async_computation.5 | async-start | bytes 1048576 | tf_op jit(solution)/shard_map/all_to_all | solution.py:159
  244.7 2.2 reshape.250
  246.9 15.8 %all-to-all-done.5 = bf16[64,2,2048]{2,1,0:T(2,128)(2,1)} async-done(((bf16[64,2,2048]{2,1,0:T(2,128)(2,1)}), bf16[64,2,2048]{2,1,0:T(2,128)(2,1)}, u32[]{:S(2)}, u32[]{:S(2)}) %all-to-all-start.5) | async-done | bytes 524320 | tf_op jit(solution)/shard_map/all_to_all | solution.py:159
  262.7 10.8 %all-to-all-start.8 = ((bf16[64,2,2048]{2,1,0:T(2,128)(2,1)}), bf16[64,2,2048]{2,1,0:T(2,128)(2,1)}, u32[]{:S(2)}, u32[]{:S(2)}) async-start(bf16[64,2,2048]{2,1,0:T(2,128)(2,1)} %reshape.250), calls=%async_computation.8 | async-start | bytes 1048576 | tf_op jit(solution)/shard_map/all_to_all | solution.py:103
  273.5 2.0 reshape.241
  278.2 2.2 reshape.242
  280.4 19.6 %all-to-all-done.8 = bf16[64,2,2048]{2,1,0:T(2,128)(2,1)} async-done(((bf16[64,2,2048]{2,1,0:T(2,128)(2,1)}), bf16[64,2,2048]{2,1,0:T(2,128)(2,1)}, u32[]{:S(2)}, u32[]{:S(2)}) %all-to-all-start.8) | async-done | bytes 524320 | tf_op jit(solution)/shard_map/all_to_all | solution.py:103
  299.9 6.6 %all-to-all-start.4 = ((bf16[64,2,2048]{2,1,0:T(2,128)(2,1)}), bf16[64,2,2048]{2,1,0:T(2,128)(2,1)}, u32[]{:S(2)}, u32[]{:S(2)}) async-start(bf16[64,2,2048]{2,1,0:T(2,128)(2,1)} %reshape.242), calls=%async_computation.4 | async-start | bytes 1048576 | tf_op jit(solution)/shard_map/all_to_all | solution.py:103
  306.6 2.0 reshape.236
  311.2 2.2 reshape.238
  313.4 16.2 %all-to-all-done.4 = bf16[64,2,2048]{2,1,0:T(2,128)(2,1)} async-done(((bf16[64,2,2048]{2,1,0:T(2,128)(2,1)}), bf16[64,2,2048]{2,1,0:T(2,128)(2,1)}, u32[]{:S(2)}, u32[]{:S(2)}) %all-to-all-start.4) | async-done | bytes 524320 | tf_op jit(solution)/shard_map/all_to_all | solution.py:103
  329.6 17.0 %all-to-all-start.2 = ((bf16[64,2,2048]{2,1,0:T(2,128)(2,1)}), bf16[64,2,2048]{2,1,0:T(2,128)(2,1)}, u32[]{:S(2)}, u32[]{:S(2)}) async-start(bf16[64,2,2048]{2,1,0:T(2,128)(2,1)} %reshape.238), calls=%async_computation.2 | async-start | bytes 1048576 | tf_op jit(solution)/shard_map/all_to_all | solution.py:103
  346.6 2.0 reshape.245
  351.6 17.3 %all-to-all-done.2 = bf16[64,2,2048]{2,1,0:T(2,128)(2,1)} async-done(((bf16[64,2,2048]{2,1,0:T(2,128)(2,1)}), bf16[64,2,2048]{2,1,0:T(2,128)(2,1)}, u32[]{:S(2)}, u32[]{:S(2)}) %all-to-all-start.2) | async-done | bytes 524320 | tf_op jit(solution)/shard_map/all_to_all | solution.py:103
  368.9 14.7 %all-to-all-start.6 = ((bf16[64,2,2048]{2,1,0:T(2,128)(2,1)}), bf16[64,2,2048]{2,1,0:T(2,128)(2,1)}, u32[]{:S(2)}, u32[]{:S(2)}) async-start(bf16[64,2,2048]{2,1,0:T(2,128)(2,1)} %reshape.246), calls=%async_computation.6 | async-start | bytes 1048576 | tf_op jit(solution)/shard_map/all_to_all | solution.py:103
  387.0 1.6 copy.95
  393.5 13.2 %all-to-all-done.6 = bf16[64,2,2048]{2,1,0:T(2,128)(2,1)} async-done(((bf16[64,2,2048]{2,1,0:T(2,128)(2,1)}), bf16[64,2,2048]{2,1,0:T(2,128)(2,1)}, u32[]{:S(2)}, u32[]{:S(2)}) %all-to-all-start.6) | async-done | bytes 524320 | tf_op jit(solution)/shard_map/all_to_all | solution.py:103
  (119 shorter events, 39.0 us)
Async XLA Ops:
  65.9 13.7 %copy-start.3 = (s32[4,4,2]{1,2,0:T(2,128)S(1)}, s32[4,4,2]{1,2,0:T(2,128)}, u32[]{:S(2)}) copy-start(s32[4,4,2]{1,2,0:T(2,128)} %param.14) | copy-start | bytes 388
  65.9 14.2 %copy-start.2 = (bf16[4,4,2048]{2,1,0:T(4,128)(2,1)S(1)}, bf16[4,4,2048]{2,1,0:T(4,128)(2,1)}, u32[]{:S(2)}) copy-start(bf16[4,4,2048]{2,1,0:T(4,128)(2,1)} %param.13) | copy-start | bytes 196612
  65.9 14.7 %copy-start.5 = (f32[2048]{0:T(1024)S(1)}, f32[2048]{0:T(1024)}, u32[]{:S(2)}) copy-start(f32[2048]{0:T(1024)} %param.12) | copy-start | bytes 24580
  69.4 29.8 %all-to-all-start = ((bf16[3,64,2,256]{3,2,0,1:T(2,128)(2,1)}), bf16[3,64,2,256]{3,2,0,1:T(2,128)(2,1)S(1)}, u32[]{:S(2)}, u32[]{:S(2)}) async-start(bf16[3,64,2,256]{3,2,0,1:T(2,128)(2,1)} %copy.80), calls=%async_computation | async-start | bytes 393216 | tf_op jit(solution)/shard_map/all_to_all | solution.py:134
  100.3 36.6 %all-to-all-start.7 = ((bf16[64,2,2048]{2,1,0:T(2,128)(2,1)}), bf16[64,2,2048]{2,1,0:T(2,128)(2,1)S(1)}, u32[]{:S(2)}, u32[]{:S(2)}) async-start(bf16[64,2,2048]{2,1,0:T(2,128)(2,1)} %bitcast.25), calls=%async_computation.7 | async-start | bytes 1048576 | tf_op jit(solution)/shard_map/all_to_all | solution.py:159
  138.0 37.0 %all-to-all-start.3 = ((bf16[64,2,2048]{2,1,0:T(2,128)(2,1)}), bf16[64,2,2048]{2,1,0:T(2,128)(2,1)S(1)}, u32[]{:S(2)}, u32[]{:S(2)}) async-start(bf16[64,2,2048]{2,1,0:T(2,128)(2,1)} %bitcast.15), calls=%async_computation.3 | async-start | bytes 1048576 | tf_op jit(solution)/shard_map/all_to_all | solution.py:159
  175.1 43.4 %copy-start = (bf16[64,2,2048]{2,1,0:T(2,128)(2,1)}, bf16[64,2,2048]{2,1,0:T(2,128)(2,1)S(1)}, u32[]{:S(2)}) copy-start(bf16[64,2,2048]{2,1,0:T(2,128)(2,1)S(1)} %all-to-all-done.3) | copy-start | bytes 1572868
  176.2 42.6 %all-to-all-start.1 = ((bf16[64,2,2048]{2,1,0:T(2,128)(2,1)}), bf16[64,2,2048]{2,1,0:T(2,128)(2,1)S(1)}, u32[]{:S(2)}, u32[]{:S(2)}) async-start(bf16[64,2,2048]{2,1,0:T(2,128)(2,1)} %bitcast.8), calls=%async_computation.1 | async-start | bytes 1048576 | tf_op jit(solution)/shard_map/all_to_all | solution.py:159
  185.3 52.2 %all-gather.3.cloned.1.call-start = ((), (), s32[]{:S(2)}) async-start(), calls=%async_computation.9 | async-start | bytes 2359296 | tf_op jit(solution)/shard_map/all_gather | solution.py:39
  218.8 18.6 %copy-start.1 = (bf16[64,2,2048]{2,1,0:T(2,128)(2,1)}, bf16[64,2,2048]{2,1,0:T(2,128)(2,1)S(1)}, u32[]{:S(2)}) copy-start(bf16[64,2,2048]{2,1,0:T(2,128)(2,1)S(1)} %all-to-all-done.1) | copy-start | bytes 1572868
  219.9 42.7 %all-to-all-start.5 = ((bf16[64,2,2048]{2,1,0:T(2,128)(2,1)}), bf16[64,2,2048]{2,1,0:T(2,128)(2,1)}, u32[]{:S(2)}, u32[]{:S(2)}) async-start(bf16[64,2,2048]{2,1,0:T(2,128)(2,1)} %bitcast.20), calls=%async_computation.5 | async-start | bytes 1048576 | tf_op jit(solution)/shard_map/all_to_all | solution.py:159
  262.7 37.2 %all-to-all-start.8 = ((bf16[64,2,2048]{2,1,0:T(2,128)(2,1)}), bf16[64,2,2048]{2,1,0:T(2,128)(2,1)}, u32[]{:S(2)}, u32[]{:S(2)}) async-start(bf16[64,2,2048]{2,1,0:T(2,128)(2,1)} %reshape.250), calls=%async_computation.8 | async-start | bytes 1048576 | tf_op jit(solution)/shard_map/all_to_all | solution.py:103
  299.9 29.7 %all-to-all-start.4 = ((bf16[64,2,2048]{2,1,0:T(2,128)(2,1)}), bf16[64,2,2048]{2,1,0:T(2,128)(2,1)}, u32[]{:S(2)}, u32[]{:S(2)}) async-start(bf16[64,2,2048]{2,1,0:T(2,128)(2,1)} %reshape.242), calls=%async_computation.4 | async-start | bytes 1048576 | tf_op jit(solution)/shard_map/all_to_all | solution.py:103
  329.6 39.3 %all-to-all-start.2 = ((bf16[64,2,2048]{2,1,0:T(2,128)(2,1)}), bf16[64,2,2048]{2,1,0:T(2,128)(2,1)}, u32[]{:S(2)}, u32[]{:S(2)}) async-start(bf16[64,2,2048]{2,1,0:T(2,128)(2,1)} %reshape.238), calls=%async_computation.2 | async-start | bytes 1048576 | tf_op jit(solution)/shard_map/all_to_all | solution.py:103
  350.1 33.5 %copy-start.4 = (f32[4,4,2]{1,2,0:T(2,128)S(1)}, f32[4,4,2]{1,2,0:T(2,128)}, u32[]{:S(2)}) copy-start(f32[4,4,2]{1,2,0:T(2,128)} %param.15) | copy-start | bytes 388
  368.9 37.9 %all-to-all-start.6 = ((bf16[64,2,2048]{2,1,0:T(2,128)(2,1)}), bf16[64,2,2048]{2,1,0:T(2,128)(2,1)}, u32[]{:S(2)}, u32[]{:S(2)}) async-start(bf16[64,2,2048]{2,1,0:T(2,128)(2,1)} %reshape.246), calls=%async_computation.6 | async-start | bytes 1048576 | tf_op jit(solution)/shard_map/all_to_all | solution.py:103
Sparse Core Ops, SparseCore 0:
  218.6 18.7 all-gather.2
where the time goes:
time: 418 us; the launch traced here: 417 us
  waiting for transfers between devices  156 us (37%)
  starting transfers between devices  101 us (24%)
  blocking collectives  88.6 us (21%)
  local copies, waits for them, and re-layouts  30.2 us (7%)
  between operations  15.1 us (4%)
  matrix products  13.4 us (3%)
  other arithmetic  12.5 us (3%)
    all_to_all x4, waiting for transfers between devices, per_device(): lax.all_to_all(copies, DP, split_axis=0, concat_axis=0, tiled=True)  70.4 us
    all_to_all x4, waiting for transfers between devices, expert_part(): lax.all_to_all(partial_out.reshape(member_count, slot_count, model_width)...  66.2 us
    psum x5, blocking collectives, by_axis(): array = lax.psum(array, axis)  56.4 us
    all_to_all x4, starting transfers between devices, expert_part(): lax.all_to_all(partial_out.reshape(member_count, slot_count, model_width)...  49.2 us
    all_to_all x4, starting transfers between devices, per_device(): lax.all_to_all(copies, DP, split_axis=0, concat_axis=0, tiled=True)  41.3 us
    all_gather x1, blocking collectives, stacked_from(): pieces = lax.all_gather(pieces, axes[k])  32.2 us
    all_to_all x1, waiting for transfers between devices, per_device(): strips = lax.all_to_all(pieces, DP, split_axis=1, concat_axis=2, tiled=True)  18.3 us
    all_to_all x1, starting transfers between devices, per_device(): strips = lax.all_to_all(pieces, DP, split_axis=1, concat_axis=2, tiled=True)  10.2 us
  transfers between devices with their start and end apart: 10, of which 9 were waited for; matrix products, arithmetic and copies ran while one was open for 11% of the time, Pallas kernels for 0%

commit v1 on v0

v1 whole, which is shorter than its diff:
```python
import math

import jax
import jax.numpy as jnp
from jax import lax
from jax.experimental import pallas as pl
from jax.experimental.pallas import tpu as pltpu
from jax.sharding import Mesh
from jax.sharding import PartitionSpec as P

DP = ("dp_0", "dp_1", "dp_2")
TENSOR = ("tensor_0", "tensor_1")
DP_TENSOR = DP + TENSOR
X_AXIS, Y_AXIS, ZH_AXIS, ZL_AXIS, C_AXIS = DP_TENSOR

MESH = pl.DeviceIdType.MESH
F32 = jnp.float32
BF16 = jnp.bfloat16

beta_one = 0.9
beta_two = 0.95
learn_rate = 0.02
decay_rate = 0.1
adam_eps = 1e-08
step_count = 10
norm_eps = 1e-06

WIDTH = 2048
PART = 256
HIDDEN = 1024
COUNT = 3 * 8 * 1024 * 2048
BLOCK = 32


def one_hot_rows(source_of):
    row = lax.broadcasted_iota(jnp.int32, (128, 128), 0)
    column = lax.broadcasted_iota(jnp.int32, (128, 128), 1)
    a, b, c, i = row // 32, (row // 8) % 4, (row // 2) % 4, row % 2
    return jnp.where(column == source_of(a, b, c, i), 1.0, 0.0).astype(BF16)


def matmul(left, right):
    return lax.dot_general(left, right, (((1,), (0,)), ((), ())), preferred_element_type=F32)


def matmul_nt(left, right):
    return lax.dot_general(left, right, (((1,), (1,)), ((), ())), preferred_element_type=F32)


def body(
    ids_ref,
    gates_ref,
    master_ref,
    one_ref,
    two_ref,
    grad_ref,
    gain_ref,
    hidden_ref,
    new_master_ref,
    new_one_ref,
    new_two_ref,
    served_ref,
    decoded_ref,
    wide,
    zrows,
    meta,
    sums_out,
    sums_in,
    stage,
    slots,
    answers,
    from_partner,
    relay,
    joined,
    back,
    parts,
    parts_in,
    wz_out,
    wz_in,
    wy_out,
    wy_in,
    wx_out,
    sum_sem,
    meta_sem,
    tok_sem,
    x_sem,
    y_sem,
    ret_sem,
    wz_sem,
    wy_sem,
    wx_sem,
    wl_sem,
    wc_sem,
):
    x = lax.axis_index(X_AXIS)
    y = lax.axis_index(Y_AXIS)
    zh = lax.axis_index(ZH_AXIS)
    zl = lax.axis_index(ZL_AXIS)
    core = lax.axis_index(C_AXIS)
    pair = y // 2
    odd = y % 2
    partner = y + 1 - 2 * odd
    other = (y + 3 + 2 * odd) % 4
    started = []

    def send(source, target, sems, index, device):
        copy = pltpu.make_async_remote_copy(
            src_ref=source,
            dst_ref=target,
            send_sem=sems.at[(0,) + index],
            recv_sem=sems.at[(1,) + index],
            device_id=device,
            device_id_type=MESH,
        )
        copy.start()
        started.append(copy)
        return copy

    def turn(axis, me, j):
        return {axis: (me + j) % 4}

    barrier = pltpu.get_barrier_semaphore()
    for axis, me in ((X_AXIS, x), (Y_AXIS, y), (ZH_AXIS, zh), (ZL_AXIS, zl)):
        for j in (1, 2, 3):
            pl.semaphore_signal(barrier, inc=1, device_id=turn(axis, me, j), device_id_type=MESH)
    pl.semaphore_signal(barrier, inc=1, device_id={C_AXIS: 1 - core}, device_id_type=MESH)

    for s in range(4):
        wide[pl.ds(4 * s, 4), :] = hidden_ref[s].astype(F32)
    rows = wide[...]
    factor = lax.rsqrt(jnp.mean(rows * rows, axis=1, keepdims=True) + norm_eps)
    zrows[zh] = (rows * factor * gain_ref[...]).astype(BF16)
    meta_row = lax.broadcasted_iota(jnp.int32, (8, 128), 0)
    meta_lane = lax.broadcasted_iota(jnp.int32, (8, 128), 1) - zh * 16
    tile = jnp.zeros((8, 128), F32)
    for s in range(4):
        for r in range(4):
            for k in range(2):
                spot = meta_lane == 4 * s + r
                tile = jnp.where(spot & (meta_row == k), ids_ref[s, r, k].astype(F32), tile)
                tile = jnp.where(spot & (meta_row == 2 + k), gates_ref[s, r, k], tile)
    meta[0] = tile
    squares = jnp.zeros((8, 128), F32)
    for block in range(12):
        values = grad_ref[pl.ds(32 * block, 32), :].astype(F32)
        values = values * values
        for i in range(4):
            for h in range(2):
                squares = squares + values[8 * i : 8 * i + 8, 128 * h : 128 * h + 128]
    sums_out[0] = squares
    pl.semaphore_wait(barrier, 13)

    phases = ((ZL_AXIS, zl), (ZH_AXIS, zh), (X_AXIS, x), (Y_AXIS, y))
    token_copies = []
    for phase, (axis, me) in enumerate(phases):
        copies = [
            send(
                sums_out.at[phase],
                sums_in.at[phase, j - 1],
                sum_sem,
                (phase, j - 1),
                turn(axis, me, j),
            )
            for j in (1, 2, 3)
        ]
        if phase == 1:
            for j in (1, 3, 2):
                token_copies.append(
                    send(meta.at[0], meta.at[j], meta_sem, (j - 1,), turn(ZH_AXIS, zh, j))
                )
                token_copies.append(
                    send(zrows.at[zh], zrows.at[zh], tok_sem, (j - 1,), turn(ZH_AXIS, zh, j))
                )
        for copy in copies:
            copy.wait_recv()
        squares = squares + sums_in[phase, 0] + sums_in[phase, 1] + sums_in[phase, 2]
        sums_out[phase + 1] = squares
    copy = send(sums_out.at[4], sums_in.at[4, 0], sum_sem, (4, 0), {C_AXIS: 1 - core})
    permute_z = one_hot_rows(lambda a, b, c, i: ((b * 4 + c) * 4 + a) * 2 + i)
    permute_y = one_hot_rows(lambda a, b, c, i: ((c * 4 + b) * 4 + a) * 2 + i)
    permute_x = one_hot_rows(lambda a, b, c, i: ((b * 4 + a) * 4 + c) * 2 + i)
    copy.wait_recv()
    squares = squares + sums_in[4, 0]
    total = jnp.sum(squares, axis=(0, 1), keepdims=True)
    clip = jnp.minimum(1.0, lax.rsqrt(total * (1.0 / COUNT) + norm_eps))

    first_fix = 1.0 / (1.0 - beta_one**step_count)
    second_fix = 1.0 / (1.0 - beta_two**step_count)
    z_copies = []
    for k in range(3):
        for half in range(4):
            at = pl.ds(128 * k + 32 * half, 32)
            scaled = grad_ref[at, :].astype(F32) * clip
            first = beta_one * one_ref[at, :] + (1.0 - beta_one) * scaled
            second = beta_two * two_ref[at, :] + (1.0 - beta_two) * scaled * scaled
            update = first * first_fix / (jnp.sqrt(second * second_fix) + adam_eps)
            old = master_ref[at, :]
            new_master_ref[at, :] = old - learn_rate * (update + decay_rate * old)
            new_one_ref[at, :] = first
            new_two_ref[at, :] = second
        rounded = new_master_ref[pl.ds(128 * k, 128), :].astype(BF16)
        wz_out[k] = matmul(permute_z, rounded).astype(BF16).reshape(4, 32, PART)
        for j in (2, 1, 3):
            z_copies.append(
                send(
                    wz_out.at[k, (zh + j) % 4],
                    wz_in.at[k, zh],
                    wz_sem,
                    (k, j - 1),
                    turn(ZH_AXIS, zh, j),
                )
            )
        wz_in[k, zh] = wz_out[k, zh]

    for copy in token_copies:
        copy.wait_recv()
    routes = meta[0] + meta[1] + meta[2] + meta[3]
    id_one, id_two = routes[0:1, 0:64], routes[1:2, 0:64]
    gate_one, gate_two = routes[2:3, 0:64], routes[3:4, 0:64]
    gate_sum = gate_one + gate_two
    share_one, share_two = gate_one / gate_sum, gate_two / gate_sum
    place = lax.broadcasted_iota(jnp.int32, (8, 64), 0)
    expert = (2 * ((x + place // 2) % 4) + (pair + place % 2) % 2).astype(F32)
    names_one = jnp.where(id_one == expert, 1.0, 0.0)
    names_two = jnp.where(id_two == expert, 1.0, 0.0)
    named = names_one + names_two
    share = names_one * share_one + names_two * share_two
    above = lax.broadcasted_iota(jnp.int32, (64, 64), 0)
    below = lax.broadcasted_iota(jnp.int32, (64, 64), 1)
    before = jnp.where((above // 4 == below // 4) & (above < below), 1.0, 0.0).astype(BF16)
    earlier = matmul(named.astype(BF16), before)
    slot_row = lax.broadcasted_iota(jnp.int32, (32, 64), 0)
    row_lane = lax.broadcasted_iota(jnp.int32, (32, 64), 1)
    same_block = jnp.where(slot_row // 2 == row_lane // 4, 1.0, 0.0)
    slot_number = (slot_row % 2).astype(F32)
    token_rows = zrows[...].reshape(64, WIDTH)
    weights = []
    x_copies = {}
    for d in (0, 2, 1, 3):
        picks = []
        for r in range(2):
            p = 2 * d + r
            hit = jnp.where(earlier[p : p + 1, :] == slot_number, same_block, 0.0)
            picks.append(hit * named[p : p + 1, :])
        chosen = matmul(jnp.concatenate(picks, axis=0).astype(BF16), token_rows)
        chosen = chosen.astype(BF16).reshape(2, BLOCK, WIDTH)
        if d == 0:
            slots[0, 0] = chosen[0]
            slots[1, 0] = chosen[1]
        else:
            stage[d - 1] = chosen
            x_copies[d] = send(
                stage.at[d - 1], slots.at[pl.ds(0, 2), d], x_sem, (0, d), turn(X_AXIS, x, d)
            )
    for p in range(8):
        hit = jnp.where(earlier[p : p + 1, :] == slot_number, same_block, 0.0)
        weights.append(hit * share[p : p + 1, :])

    y_copies = []
    for k in range(3):
        for copy in z_copies[3 * k : 3 * k + 3]:
            copy.wait_recv()
        gathered = wz_in[k].reshape(128, PART)
        wy_out[k] = matmul(permute_y, gathered).astype(BF16).reshape(4, 32, PART)
        for j in (2, 1, 3):
            y_copies.append(
                send(
                    wy_out.at[k, (y + j) % 4],
                    wy_in.at[k, y],
                    wy_sem,
                    (k, j - 1),
                    turn(Y_AXIS, y, j),
                )
            )
        wy_in[k, y] = wy_out[k, y]

    to_partner, to_other, onward = {}, {}, {}
    order = (0, 1, 3, 2)

    def spread(d):
        if d:
            x_copies[d].wait_recv()
        to_other[d] = send(
            slots.at[1, d], slots.at[3, d], y_sem, (1, d), {Y_AXIS: other}
        )
        to_partner[d] = send(
            slots.at[0, d], slots.at[2, d], y_sem, (0, d), {Y_AXIS: partner}
        )

    def forward(d):
        to_other[d].wait_recv()
        onward[d] = send(slots.at[3, d], slots.at[4, d], y_sem, (2, d), {Y_AXIS: partner})

    spread(0)
    t = (2 * zl + core) * PART
    columns = pl.ds(pl.multiple_of(t, PART), PART)
    own_rows = pl.ds(pl.multiple_of(32 * x, 32), 32)
    wx_copies = []
    for k in range(3):
        for copy in y_copies[3 * k : 3 * k + 3]:
            copy.wait_recv()
        gathered = wy_in[k].reshape(128, PART)
        wx_out[k] = matmul(permute_x, gathered).astype(BF16).reshape(4, 32, PART)
        for j in (2, 1, 3):
            wx_copies.append(
                send(
                    wx_out.at[k, (x + j) % 4],
                    served_ref.at[k, own_rows, columns],
                    wx_sem,
                    (k, j - 1),
                    turn(X_AXIS, x, j),
                )
            )
        served_ref[k, own_rows, columns] = wx_out[k, x]

    line_copies = []
    core_copies = []
    for k in range(3):
        for copy in wx_copies[3 * k : 3 * k + 3]:
            copy.wait_recv()
        mine = served_ref.at[k, :, columns]
        for j in (1, 3, 2):
            line_copies.append((k, j, send(mine, mine, wl_sem, (k, j - 1), turn(ZL_AXIS, zl, j))))
        core_copies.append(send(mine, mine, wc_sem, (k, 0), {C_AXIS: 1 - core}))
    spread(1)
    forward(0)
    spread(3)
    forward(1)
    spread(2)
    forward(3)
    for k, j, copy in line_copies:
        copy.wait_recv()
        theirs = (2 * ((zl + 4 - j) % 4) + core) * PART
        piece = served_ref.at[k, :, pl.ds(pl.multiple_of(theirs, PART), PART)]
        core_copies.append(send(piece, piece, wc_sem, (k, j), {C_AXIS: 1 - core}))
    forward(2)
    for copy in core_copies:
        copy.wait_recv()
    for d in order:
        to_partner[d].wait_recv()
        onward[d].wait_recv()

    for number, origin in ((3, 4), (1, 2), (2, 3), (0, 0)):
        taken = slots[origin].reshape(4 * BLOCK, WIDTH)
        gate = matmul_nt(taken, served_ref[0]) * (1.0 / math.sqrt(WIDTH))
        up = matmul_nt(taken, served_ref[1]) * (1.0 / math.sqrt(WIDTH))
        active = (gate / (1.0 + jnp.exp(-gate)) * up).astype(BF16)
        for h in range(4):
            span = pl.ds(512 * h, 512)
            out = matmul(active, served_ref[2, :, span]) * (1.0 / math.sqrt(HIDDEN))
            answers[number, :, :, span] = out.astype(BF16).reshape(4, BLOCK, 512)
        if number == 3 or number == 1:
            for d in (2, 1, 3, 0):
                started_copy = send(
                    answers.at[number, d],
                    from_partner.at[number // 2, d],
                    ret_sem,
                    (number // 2, d),
                    {Y_AXIS: partner},
                )
                if number == 3:
                    to_other[d] = started_copy
                else:
                    to_partner[d] = started_copy

    for d in (2, 1, 3, 0):
        to_other[d].wait_recv()
        both = answers[2, d].astype(F32) + from_partner[1, d].astype(F32)
        relay[d] = both.astype(BF16)
        onward[d] = send(relay.at[d], joined.at[1, d], ret_sem, (2, d), {Y_AXIS: other})
    for d in (2, 1, 3, 0):
        to_partner[d].wait_recv()
        both = answers[0, d].astype(F32) + from_partner[0, d].astype(F32)
        joined[0, d] = both.astype(BF16)
        onward[d].wait_recv()
        if d:
            x_copies[d] = send(
                joined.at[pl.ds(0, 2), d], back.at[d - 1], x_sem, (1, d), turn(X_AXIS, x, 4 - d)
            )

    parted = []
    for d in range(4):
        weight = jnp.concatenate(weights[2 * d : 2 * d + 2], axis=0).T
        high = weight.astype(BF16)
        rest = weight - high.astype(F32)
        middle = rest.astype(BF16)
        low = (rest - middle.astype(F32)).astype(BF16)
        parted.append((high, middle, low))
    gathered_rows = jnp.zeros((64, WIDTH), F32)
    for d in (0, 1, 3, 2):
        if d:
            x_copies[d].wait_recv()
            held = back[d - 1].reshape(2 * BLOCK, WIDTH)
        else:
            held = joined[:, 0].reshape(2 * BLOCK, WIDTH)
        for piece in parted[d]:
            gathered_rows = gathered_rows + matmul(piece, held)
    parts[...] = gathered_rows.astype(BF16).reshape(4, 16, WIDTH)
    z_back = [
        send(parts.at[(zh + j) % 4], parts_in.at[j - 1], ret_sem, (3, j - 1), turn(ZH_AXIS, zh, j))
        for j in (2, 1, 3)
    ]
    result = wide[...] + parts[zh].astype(F32)
    for copy in z_back:
        copy.wait_recv()
    for j in range(3):
        result = result + parts_in[j].astype(F32)
    wide[...] = result
    for s in range(4):
        decoded_ref[s] = wide[pl.ds(4 * s, 4), :].astype(BF16)
    for copy in started:
        copy.wait_send()


def per_device(
    master, moment_one, moment_two, gradients, norm_gain, hidden_in, expert_ids, route_weights
):
    vmem = pl.BlockSpec(memory_space=pltpu.VMEM)
    smem = pl.BlockSpec(memory_space=pltpu.SMEM)
    flat = (384, PART)
    dma = pltpu.SemaphoreType.DMA
    new_master, new_one, new_two, served, decoded = pl.pallas_call(
        body,
        out_shape=(
            jax.ShapeDtypeStruct(flat, F32),
            jax.ShapeDtypeStruct(flat, F32),
            jax.ShapeDtypeStruct(flat, F32),
            jax.ShapeDtypeStruct((3, 128, WIDTH), BF16),
            jax.ShapeDtypeStruct((4, 4, WIDTH), BF16),
        ),
        in_specs=[smem, smem] + [vmem] * 6,
        out_specs=(vmem,) * 5,
        scratch_shapes=[
            pltpu.VMEM((16, WIDTH), F32),
            pltpu.VMEM((4, 16, WIDTH), BF16),
            pltpu.VMEM((4, 8, 128), F32),
            pltpu.VMEM((5, 8, 128), F32),
            pltpu.VMEM((5, 3, 8, 128), F32),
            pltpu.VMEM((3, 2, BLOCK, WIDTH), BF16),
            pltpu.VMEM((5, 4, BLOCK, WIDTH), BF16),
            pltpu.VMEM((4, 4, BLOCK, WIDTH), BF16),
            pltpu.VMEM((2, 4, BLOCK, WIDTH), BF16),
            pltpu.VMEM((4, BLOCK, WIDTH), BF16),
            pltpu.VMEM((2, 4, BLOCK, WIDTH), BF16),
            pltpu.VMEM((3, 2, BLOCK, WIDTH), BF16),
            pltpu.VMEM((4, 16, WIDTH), BF16),
            pltpu.VMEM((3, 16, WIDTH), BF16),
            pltpu.VMEM((3, 4, 32, PART), BF16),
            pltpu.VMEM((3, 4, 32, PART), BF16),
            pltpu.VMEM((3, 4, 32, PART), BF16),
            pltpu.VMEM((3, 4, 32, PART), BF16),
            pltpu.VMEM((3, 4, 32, PART), BF16),
            dma((2, 5, 3)),
            dma((2, 3)),
            dma((2, 3)),
            dma((2, 2, 4)),
            dma((2, 3, 4)),
            dma((2, 4, 4)),
            dma((2, 3, 3)),
            dma((2, 3, 3)),
            dma((2, 3, 3)),
            dma((2, 3, 3)),
            dma((2, 3, 4)),
        ],
        compiler_params=pltpu.CompilerParams(
            collective_id=0, has_side_effects=True, vmem_limit_bytes=48 * 1024 * 1024
        ),
        name="step",
    )(
        expert_ids,
        route_weights,
        master.reshape(flat),
        moment_one.reshape(flat),
        moment_two.reshape(flat),
        gradients.reshape(flat),
        norm_gain.reshape(1, WIDTH),
        hidden_in,
    )
    return (
        new_master.reshape(master.shape),
        new_one.reshape(master.shape),
        new_two.reshape(master.shape),
        served,
        decoded,
    )


def solution(mesh):
    split = Mesh(mesh.devices.reshape(4, 4, 4, 4, 2), DP_TENSOR)
    sharded = P(None, None, DP, TENSOR)
    by_row = P(None, DP_TENSOR, None)
    return jax.shard_map(
        per_device,
        mesh=split,
        in_specs=(sharded, sharded, sharded, sharded, P(), by_row, by_row, by_row),
        out_specs=(sharded, sharded, sharded, P(None, DP, None), by_row),
        check_vma=False,
    )
```

time: 418 us -> 136 us (0.33)
  the two profiles are of different devices: /device:TPU:2 before, /device:TPU:1 now
where the time goes in v1:
time: 136 us; the launch traced here: 135 us
  Pallas kernels  124 us (91%)
  local copies, waits for them, and re-layouts  11 us (8%)
    pallas_call x1, Pallas kernels, per_device(): pl.pallas_call(body, out_shape=(jax.ShapeDtypeStruct(flat, F32), jax.Shap...  124 us
    unnamed x19, local copies, waits for them, and re-layouts  11 us

profile of v1, /device:TPU:1, one launch (start us, length us, event | category | flops | bytes accessed | tf_op | source)
XLA Modules:
  0.0 135.5 jit_solution(2239847853317274390)
XLA Ops:
  0.6 0.8 copy.13.ids_ref
  1.4 0.8 copy.14.gates_ref
  2.2 0.0 copy-start
  2.2 1.0 copy-done
  3.2 0.0 copy-start.1
  3.2 1.0 copy-done.1
  4.2 0.0 copy-start.2
  4.2 1.0 copy-done.2
  5.2 0.0 copy-start.3
  5.2 0.9 copy-done.3
  6.1 0.0 copy-start.4
  6.1 0.8 copy-done.4
  7.0 0.0 copy-start.5
  7.0 0.7 copy-done.5
  7.7 123.8 %step.1 = (f32[384,256]{1,0:T(8,128)S(1)}, f32[384,256]{1,0:T(8,128)S(1)}, f32[384,256]{1,0:T(8,128)S(1)}, bf16[3,128,2048]{2,1,0:T(8,128)(2,1)S(1)}, bf16[4,4,2048]{2,1,0:T(4,128)(2,1)S(1)}) custom-call(s32[4,4,2]{2,1,0:T(4,128)S(1)} %copy.13.ids_ref, f32[4,4,2]{2,1,0:T(4,128)S(1)} %copy.14.gates_ref, f32[384,256]{1,0:T(8,128)S(1)} %bitcast.11, ...), custom_call_target="tpu_custom_call" | custom-call | tf_op jit(solution)/shard_map/step/pallas_call | solution.py:422
  131.5 0.7 copy.20
  132.2 0.7 copy.21
  133.0 0.7 copy.22
  133.7 1.1 copy.23
  134.9 0.6 copy.24
Async XLA Ops:
  2.2 1.0 copy-start
  3.2 1.0 copy-start.1
  4.2 1.0 copy-start.2
  5.2 0.9 copy-start.3
  6.1 0.8 copy-start.4
  7.0 0.7 copy-start.5

commit v2 on v1

v2 whole, which is shorter than its diff:
```python
import math

import jax
import jax.numpy as jnp
from jax import lax
from jax.experimental import pallas as pl
from jax.experimental.pallas import tpu as pltpu
from jax.sharding import Mesh
from jax.sharding import PartitionSpec as P

DP = ("dp_0", "dp_1", "dp_2")
TENSOR = ("tensor_0", "tensor_1")
DP_TENSOR = DP + TENSOR
X_AXIS, Y_AXIS, ZH_AXIS, ZL_AXIS, C_AXIS = DP_TENSOR

MESH = pl.DeviceIdType.MESH
F32 = jnp.float32
BF16 = jnp.bfloat16

beta_one = 0.9
beta_two = 0.95
learn_rate = 0.02
decay_rate = 0.1
adam_eps = 1e-08
step_count = 10
norm_eps = 1e-06

WIDTH = 2048
PART = 256
HIDDEN = 1024
COUNT = 3 * 8 * 1024 * 2048
BLOCK = 32


def one_hot_rows(source_of):
    row = lax.broadcasted_iota(jnp.int32, (128, 128), 0)
    column = lax.broadcasted_iota(jnp.int32, (128, 128), 1)
    a, b, c, i = row // 32, (row // 8) % 4, (row // 2) % 4, row % 2
    return jnp.where(column == source_of(a, b, c, i), 1.0, 0.0).astype(BF16)


def matmul(left, right):
    return lax.dot_general(left, right, (((1,), (0,)), ((), ())), preferred_element_type=F32)


def matmul_nt(left, right):
    return lax.dot_general(left, right, (((1,), (1,)), ((), ())), preferred_element_type=F32)


def body(
    ids_ref,
    gates_ref,
    master_hbm,
    one_hbm,
    two_hbm,
    grad_hbm,
    gain_hbm,
    hidden_hbm,
    new_master_hbm,
    new_one_hbm,
    new_two_hbm,
    served_hbm,
    decoded_hbm,
    new_master_ref,
    new_one_ref,
    new_two_ref,
    decoded_ref,
    master_ref,
    one_ref,
    two_ref,
    grad_ref,
    gain_ref,
    hidden_ref,
    wide,
    zrows,
    meta,
    sums_out,
    sums_in,
    stage,
    slots,
    answers,
    from_core,
    relay,
    joined,
    back,
    parts,
    parts_in,
    wz_out,
    wz_in,
    wy_out,
    wy_in,
    wx_out,
    wall,
    in_sem,
    out_sem,
    sum_sem,
    meta_sem,
    tok_sem,
    x_sem,
    y_sem,
    core_sem,
    ret_sem,
    back_sem,
    end_sem,
    wz_sem,
    wy_sem,
    wx_sem,
    wl_sem,
    wc_sem,
    wp_sem,
):
    x = lax.axis_index(X_AXIS)
    y = lax.axis_index(Y_AXIS)
    zh = lax.axis_index(ZH_AXIS)
    zl = lax.axis_index(ZL_AXIS)
    core = lax.axis_index(C_AXIS)
    pair = y // 2
    odd = y % 2
    partner = y + 1 - 2 * odd
    other = (y + 3 + 2 * odd) % 4
    next_core = {C_AXIS: 1 - core}
    started = []

    def send(source, target, sems, index, device):
        copy = pltpu.make_async_remote_copy(
            src_ref=source,
            dst_ref=target,
            send_sem=sems.at[(0,) + index],
            recv_sem=sems.at[(1,) + index],
            device_id=device,
            device_id_type=MESH,
        )
        copy.start()
        started.append(copy)
        return copy

    def turn(axis, me, j):
        return {axis: (me + j) % 4}

    def along_z(j):
        z = (4 * zh + zl + j) % 16
        return {ZH_AXIS: z // 4, ZL_AXIS: z % 4}

    barrier = pltpu.get_barrier_semaphore()
    peers = [along_z(j) for j in (8, 7, 9, 6, 10, 5, 11, 4, 12, 3, 13, 2, 14, 1, 15)]
    peers += [turn(axis, me, j) for axis, me in ((X_AXIS, x), (Y_AXIS, y)) for j in (2, 1, 3)]
    peers += [{Y_AXIS: partner, C_AXIS: 1 - core}, next_core]
    for peer in peers:
        pl.semaphore_signal(barrier, inc=1, device_id=peer, device_id_type=MESH)
    loads = [
        pltpu.make_async_copy(source, target, in_sem.at[number])
        for number, (source, target) in enumerate(
            (
                (hidden_hbm, hidden_ref),
                (gain_hbm, gain_ref),
                (grad_hbm, grad_ref),
                (master_hbm, master_ref),
                (one_hbm, one_ref),
                (two_hbm, two_ref),
            )
        )
    ]
    for load in loads:
        load.start()

    meta_row = lax.broadcasted_iota(jnp.int32, (8, 128), 0)
    meta_lane = lax.broadcasted_iota(jnp.int32, (8, 128), 1) - zh * 8
    tile = jnp.zeros((8, 128), F32)
    for s in range(4):
        for r in range(4):
            spot = meta_lane == 32 * (s // 2) + 4 * (s % 2) + r
            for k in range(2):
                tile = jnp.where(spot & (meta_row == k), ids_ref[s, k, r].astype(F32), tile)
                tile = jnp.where(spot & (meta_row == 2 + k), gates_ref[s, k, r], tile)
    meta[0] = tile
    loads[0].wait()
    loads[1].wait()
    for s in range(4):
        wide[pl.ds(4 * s, 4), :] = hidden_ref[s].astype(F32)
    rows = wide[...]
    factor = lax.rsqrt(jnp.mean(rows * rows, axis=1, keepdims=True) + norm_eps)
    normed = rows * factor * gain_ref[...]
    zrows[0, zh] = normed[0:8].astype(BF16)
    zrows[1, zh] = normed[8:16].astype(BF16)
    loads[2].wait()
    squares = jnp.zeros((8, 128), F32)
    for block in range(12):
        values = grad_ref[pl.ds(32 * block, 32), :].astype(F32)
        values = values * values
        for i in range(4):
            for h in range(2):
                squares = squares + values[8 * i : 8 * i + 8, 128 * h : 128 * h + 128]
    sums_out[0] = squares
    pl.semaphore_wait(barrier, len(peers))

    slot = 0
    token_copies = []
    for phase, devices in enumerate(
        (
            [along_z(j) for j in (8, 7, 9, 6, 10, 5, 11, 4, 12, 3, 13, 2, 14, 1, 15)],
            [turn(X_AXIS, x, j) for j in (2, 1, 3)],
            [turn(Y_AXIS, y, j) for j in (2, 1, 3)],
            [next_core],
        )
    ):
        copies = [
            send(sums_out.at[phase], sums_in.at[slot + i], sum_sem, (slot + i,), device)
            for i, device in enumerate(devices)
        ]
        if phase == 0:
            for j in (2, 1, 3):
                token_copies.append(
                    send(meta.at[0], meta.at[j], meta_sem, (j - 1,), turn(ZH_AXIS, zh, j))
                )
                token_copies.append(
                    send(zrows.at[:, zh], zrows.at[:, zh], tok_sem, (j - 1,), turn(ZH_AXIS, zh, j))
                )
        if phase == 3:
            permute_z = one_hot_rows(lambda a, b, c, i: ((b * 4 + c) * 4 + a) * 2 + i)
            permute_y = one_hot_rows(lambda a, b, c, i: ((c * 4 + b) * 4 + a) * 2 + i)
            permute_x = one_hot_rows(lambda a, b, c, i: ((b * 4 + a) * 4 + c) * 2 + i)
            for load in loads[3:]:
                load.wait()
        for i, copy in enumerate(copies):
            copy.wait_recv()
            squares = squares + sums_in[slot + i]
        slot += len(copies)
        if phase < 3:
            sums_out[phase + 1] = squares
    total = jnp.sum(squares, axis=(0, 1), keepdims=True)
    clip = jnp.minimum(1.0, lax.rsqrt(total * (1.0 / COUNT) + norm_eps))

    first_fix = 1.0 / (1.0 - beta_one**step_count)
    second_fix = 1.0 / (1.0 - beta_two**step_count)
    z_copies = []
    stores = []

    def keep(source, target):
        copy = pltpu.make_async_copy(source, target, out_sem.at[len(stores)])
        copy.start()
        stores.append(copy)

    for k in range(3):
        for block in range(4):
            at = pl.ds(128 * k + 32 * block, 32)
            scaled = grad_ref[at, :].astype(F32) * clip
            first = beta_one * one_ref[at, :] + (1.0 - beta_one) * scaled
            second = beta_two * two_ref[at, :] + (1.0 - beta_two) * scaled * scaled
            update = first * first_fix / (jnp.sqrt(second * second_fix) + adam_eps)
            old = master_ref[at, :]
            new_master_ref[at, :] = old - learn_rate * (update + decay_rate * old)
            new_one_ref[at, :] = first
            new_two_ref[at, :] = second
        rounded = new_master_ref[pl.ds(128 * k, 128), :].astype(BF16)
        wz_out[k] = matmul(permute_z, rounded).astype(BF16).reshape(4, 32, PART)
        for j in (2, 1, 3):
            z_copies.append(
                send(
                    wz_out.at[k, (zh + j) % 4],
                    wz_in.at[k, zh],
                    wz_sem,
                    (k, j - 1),
                    turn(ZH_AXIS, zh, j),
                )
            )
        wz_in[k, zh] = wz_out[k, zh]
    keep(new_master_ref, new_master_hbm)
    keep(new_one_ref, new_one_hbm)
    keep(new_two_ref, new_two_hbm)

    for copy in token_copies:
        copy.wait_recv()
    routes = meta[0] + meta[1] + meta[2] + meta[3]
    id_one, id_two = routes[0:1, 0:64], routes[1:2, 0:64]
    gate_one, gate_two = routes[2:3, 0:64], routes[3:4, 0:64]
    gate_sum = gate_one + gate_two
    share_one, share_two = gate_one / gate_sum, gate_two / gate_sum
    place = lax.broadcasted_iota(jnp.int32, (8, 64), 0)
    expert = (2 * ((x + place // 2) % 4) + (pair + place % 2) % 2).astype(F32)
    names_one = jnp.where(id_one == expert, 1.0, 0.0)
    names_two = jnp.where(id_two == expert, 1.0, 0.0)
    named = names_one + names_two
    share = names_one * share_one + names_two * share_two
    above = lax.broadcasted_iota(jnp.int32, (64, 64), 0)
    below = lax.broadcasted_iota(jnp.int32, (64, 64), 1)
    before = jnp.where((above // 4 == below // 4) & (above < below), 1.0, 0.0).astype(BF16)
    earlier = matmul(named.astype(BF16), before)
    slot_row = lax.broadcasted_iota(jnp.int32, (32, 64), 0)
    row_lane = lax.broadcasted_iota(jnp.int32, (32, 64), 1)
    same_block = jnp.where(slot_row // 2 == row_lane // 4, 1.0, 0.0)
    slot_number = (slot_row % 2).astype(F32)
    hits = [jnp.where(earlier[p : p + 1, :] == slot_number, same_block, 0.0) for p in range(8)]
    token_rows = zrows[...].reshape(64, WIDTH)
    x_copies = {}
    for d in (0, 2, 1, 3):
        picks = [hits[2 * d + r] * named[2 * d + r : 2 * d + r + 1, :] for r in (1, 0)]
        chosen = matmul(jnp.concatenate(picks, axis=0).astype(BF16), token_rows)
        chosen = chosen.astype(BF16).reshape(2, BLOCK, WIDTH)
        if d == 0:
            slots[0, 0] = chosen[0]
            slots[1, 0] = chosen[1]
        else:
            stage[d - 1] = chosen
            x_copies[d] = send(
                stage.at[d - 1], slots.at[pl.ds(0, 2), d], x_sem, (d - 1,), turn(X_AXIS, x, d)
            )
    weights = []
    for h in range(2):
        columns = [hits[p] * share[p : p + 1, :] for p in range(8)]
        columns = [c[16 * h : 16 * h + 16, 32 * h : 32 * h + 32] for c in columns]
        weight = jnp.concatenate(columns, axis=0).T
        high = weight.astype(BF16)
        rest = weight - high.astype(F32)
        middle = rest.astype(BF16)
        low = (rest - middle.astype(F32)).astype(BF16)
        weights.append((high, middle, low))

    y_copies = []
    for k in range(3):
        for copy in z_copies[3 * k : 3 * k + 3]:
            copy.wait_recv()
        gathered = wz_in[k].reshape(128, PART)
        wy_out[k] = matmul(permute_y, gathered).astype(BF16).reshape(4, 32, PART)
        for j in (2, 1, 3):
            y_copies.append(
                send(
                    wy_out.at[k, (y + j) % 4],
                    wy_in.at[k, y],
                    wy_sem,
                    (k, j - 1),
                    turn(Y_AXIS, y, j),
                )
            )
        wy_in[k, y] = wy_out[k, y]

    over_y, over_core = {}, []

    def spread(d):
        if d:
            x_copies[d].wait_recv()
        over_y[d] = send(slots.at[0, d], slots.at[3, d], y_sem, (d,), {Y_AXIS: other})
        over_core.append(send(slots.at[1, d], slots.at[2, d], core_sem, (0, d), next_core))

    def forward(d):
        over_y[d].wait_recv()
        over_core.append(send(slots.at[3, d], slots.at[4, d], core_sem, (1, d), next_core))

    spread(0)

    def columns_of(position):
        return pl.ds(pl.multiple_of((2 * position + core) * PART, PART), PART)

    own_rows = pl.ds(pl.multiple_of(32 * x, 32), 32)
    wx_copies = []
    for k in range(3):
        for copy in y_copies[3 * k : 3 * k + 3]:
            copy.wait_recv()
        gathered = wy_in[k].reshape(128, PART)
        wx_out[k] = matmul(permute_x, gathered).astype(BF16).reshape(4, 32, PART)
        for j in (2, 1, 3):
            wx_copies.append(
                send(
                    wx_out.at[k, (x + j) % 4],
                    wall.at[odd, k, own_rows, columns_of(zl)],
                    wx_sem,
                    (k, j - 1),
                    turn(X_AXIS, x, j),
                )
            )
        wall[odd, k, own_rows, columns_of(zl)] = wx_out[k, x]

    across = {Y_AXIS: partner, C_AXIS: odd}
    line_copies = []
    core_copies = []

    def share_out(k, j, position):
        piece = wall.at[odd, k, :, columns_of(position)]
        send(piece, piece, wp_sem, (k, 2 * j + core), across)
        core_copies.append(send(piece, piece, wc_sem, (k, j), next_core))

    for k in range(3):
        for copy in wx_copies[3 * k : 3 * k + 3]:
            copy.wait_recv()
        mine = wall.at[odd, k, :, columns_of(zl)]
        for j in (2, 1, 3):
            line_copies.append((k, j, send(mine, mine, wl_sem, (k, j - 1), turn(ZL_AXIS, zl, j))))
        share_out(k, 0, zl)
    spread(1)
    forward(0)
    spread(3)
    forward(1)
    spread(2)
    for k, j, copy in line_copies:
        copy.wait_recv()
        share_out(k, j, (zl + 4 - j) % 4)
    forward(3)
    forward(2)
    for copy in core_copies:
        copy.wait_recv()
    keep(wall.at[odd], served_hbm)
    for copy in over_core:
        copy.wait_recv()

    @pl.when(core != odd)
    def _():
        for k in range(3):
            for number in range(8):
                piece = wall.at[core, k, :, pl.ds(PART * number, PART)]
                pltpu.make_async_remote_copy(
                    src_ref=piece,
                    dst_ref=piece,
                    send_sem=wp_sem.at[0, k, number],
                    recv_sem=wp_sem.at[1, k, number],
                    device_id=across,
                    device_id_type=MESH,
                ).wait_recv()

    into = wall.at[core, pl.ds(0, 2)]
    swaps = []
    for h in range(2):
        taken = slots[pl.ds(1, 4), :, pl.ds(16 * h, 16), :].reshape(256, WIDTH)
        projected = matmul_nt(taken, into[...].reshape(256, WIDTH)) * (1.0 / math.sqrt(WIDTH))
        gate, up = projected[:, :128], projected[:, 128:]
        active = (gate / (1.0 + jnp.exp(-gate)) * up).astype(BF16)
        for i in range(4):
            span = pl.ds(512 * i, 512)
            out = matmul(active, wall[core, 2, :, span]) * (1.0 / math.sqrt(HIDDEN))
            answers[h, :, :, :, span] = out.astype(BF16).reshape(4, 4, 16, 512)
        for number in (3, 1):
            swaps.append(
                send(
                    answers.at[h, number],
                    from_core.at[h, number // 2],
                    ret_sem,
                    (h, number // 2),
                    next_core,
                )
            )

    over_y = []
    for h in range(2):
        swaps[2 * h].wait_recv()
        relay[h] = (answers[h, 2].astype(F32) + from_core[h, 1].astype(F32)).astype(BF16)
        over_y.append(send(relay.at[h], joined.at[h, 1], ret_sem, (h, 2), {Y_AXIS: other}))
        swaps[2 * h + 1].wait_recv()
        joined[h, 0] = (answers[h, 0].astype(F32) + from_core[h, 0].astype(F32)).astype(BF16)
    over_x = []
    for h in range(2):
        over_y[h].wait_recv()
        for d in (2, 1, 3):
            over_x.append(
                send(joined.at[h, :, d], back.at[h, d], back_sem, (h, d), turn(X_AXIS, x, 4 - d))
            )
        back[h, 0] = joined[h, :, 0]

    over_z = []
    for h in range(2):
        for copy in over_x[3 * h : 3 * h + 3]:
            copy.wait_recv()
        held = back[h].reshape(128, WIDTH)
        made = matmul(weights[h][0], held) + matmul(weights[h][1], held) + matmul(weights[h][2], held)
        made = made.reshape(4, 8, WIDTH)
        parts[h] = made.astype(BF16)
        for j in (2, 1, 3):
            over_z.append(
                send(
                    parts.at[h, (zh + j) % 4],
                    parts_in.at[h, j - 1],
                    end_sem,
                    (h, j - 1),
                    turn(ZH_AXIS, zh, j),
                )
            )
    for h in range(2):
        result = wide[pl.ds(8 * h, 8), :] + parts[h, zh].astype(F32)
        for copy in over_z[3 * h : 3 * h + 3]:
            copy.wait_recv()
        for j in range(3):
            result = result + parts_in[h, j].astype(F32)
        decoded_ref[2 * h] = result[0:4].astype(BF16)
        decoded_ref[2 * h + 1] = result[4:8].astype(BF16)
    keep(decoded_ref, decoded_hbm)
    for copy in stores:
        copy.wait()
    for copy in started:
        copy.wait_send()


def hand_out(*refs):
    sources, targets, held, in_sem, out_sem = refs[:5], refs[5:10], refs[10:15], refs[15], refs[16]
    pieces = [(i, ()) for i in (0, 1, 2)] + [(3, (k,)) for k in range(3)] + [(4, ())]

    def piece(refs, i, at):
        return refs[i].at[at] if at else refs[i]

    loads, stores = [], []
    for number, (i, at) in enumerate(pieces):
        loads.append(
            pltpu.make_async_copy(piece(sources, i, at), piece(held, i, at), in_sem.at[number])
        )
        loads[-1].start()
    for number, (i, at) in enumerate(pieces):
        loads[number].wait()
        stores.append(
            pltpu.make_async_copy(piece(held, i, at), piece(targets, i, at), out_sem.at[number])
        )
        stores[-1].start()
    for store in stores:
        store.wait()


def per_device(
    master, moment_one, moment_two, gradients, norm_gain, hidden_in, expert_ids, route_weights
):
    smem = pl.BlockSpec(memory_space=pltpu.SMEM)
    anywhere = pl.BlockSpec(memory_space=pltpu.HBM)
    flat = (384, PART)
    dma = pltpu.SemaphoreType.DMA
    out_shape = (
        jax.ShapeDtypeStruct(flat, F32),
        jax.ShapeDtypeStruct(flat, F32),
        jax.ShapeDtypeStruct(flat, F32),
        jax.ShapeDtypeStruct((3, 128, WIDTH), BF16),
        jax.ShapeDtypeStruct((4, 4, WIDTH), BF16),
    )
    results = pl.pallas_call(
        body,
        out_shape=out_shape,
        in_specs=[smem, smem] + [anywhere] * 6,
        out_specs=(anywhere,) * 5,
        scratch_shapes=[
            pltpu.VMEM(flat, F32),
            pltpu.VMEM(flat, F32),
            pltpu.VMEM(flat, F32),
            pltpu.VMEM((4, 4, WIDTH), BF16),
            pltpu.VMEM(flat, F32),
            pltpu.VMEM(flat, F32),
            pltpu.VMEM(flat, F32),
            pltpu.VMEM(flat, BF16),
            pltpu.VMEM((1, WIDTH), F32),
            pltpu.VMEM((4, 4, WIDTH), BF16),
            pltpu.VMEM((16, WIDTH), F32),
            pltpu.VMEM((2, 4, 8, WIDTH), BF16),
            pltpu.VMEM((4, 8, 128), F32),
            pltpu.VMEM((4, 8, 128), F32),
            pltpu.VMEM((22, 8, 128), F32),
            pltpu.VMEM((3, 2, BLOCK, WIDTH), BF16),
            pltpu.VMEM((5, 4, BLOCK, WIDTH), BF16),
            pltpu.VMEM((2, 4, 4, 16, WIDTH), BF16),
            pltpu.VMEM((2, 2, 4, 16, WIDTH), BF16),
            pltpu.VMEM((2, 4, 16, WIDTH), BF16),
            pltpu.VMEM((2, 2, 4, 16, WIDTH), BF16),
            pltpu.VMEM((2, 4, 2, 16, WIDTH), BF16),
            pltpu.VMEM((2, 4, 8, WIDTH), BF16),
            pltpu.VMEM((2, 3, 8, WIDTH), BF16),
            pltpu.VMEM((3, 4, 32, PART), BF16),
            pltpu.VMEM((3, 4, 32, PART), BF16),
            pltpu.VMEM((3, 4, 32, PART), BF16),
            pltpu.VMEM((3, 4, 32, PART), BF16),
            pltpu.VMEM((3, 4, 32, PART), BF16),
            pltpu.VMEM((2, 3, 128, WIDTH), BF16),
            dma((6,)),
            dma((5,)),
            dma((2, 22)),
            dma((2, 3)),
            dma((2, 3)),
            dma((2, 3)),
            dma((2, 4)),
            dma((2, 2, 4)),
            dma((2, 2, 3)),
            dma((2, 2, 4)),
            dma((2, 2, 3)),
            dma((2, 3, 3)),
            dma((2, 3, 3)),
            dma((2, 3, 3)),
            dma((2, 3, 3)),
            dma((2, 3, 4)),
            dma((2, 3, 8)),
        ],
        compiler_params=pltpu.CompilerParams(
            collective_id=0, has_side_effects=True, vmem_limit_bytes=56 * 1024 * 1024
        ),
        name="step",
    )(
        expert_ids.transpose(0, 2, 1),
        route_weights.transpose(0, 2, 1),
        master.reshape(flat),
        moment_one.reshape(flat),
        moment_two.reshape(flat),
        gradients.reshape(flat),
        norm_gain.reshape(1, WIDTH),
        hidden_in,
    )
    new_master, new_one, new_two, served, decoded = pl.pallas_call(
        hand_out,
        out_shape=out_shape,
        in_specs=[anywhere] * 5,
        out_specs=(anywhere,) * 5,
        scratch_shapes=[pltpu.VMEM(array.shape, array.dtype) for array in out_shape]
        + [dma((7,)), dma((7,))],
        name="hand_out",
    )(*results)
    return (
        new_master.reshape(master.shape),
        new_one.reshape(master.shape),
        new_two.reshape(master.shape),
        served,
        decoded,
    )


def solution(mesh):
    split = Mesh(mesh.devices.reshape(4, 4, 4, 4, 2), DP_TENSOR)
    sharded = P(None, None, DP, TENSOR)
    by_row = P(None, DP_TENSOR, None)
    return jax.shard_map(
        per_device,
        mesh=split,
        in_specs=(sharded, sharded, sharded, sharded, P(), by_row, by_row, by_row),
        out_specs=(sharded, sharded, sharded, P(None, DP, None), by_row),
        check_vma=False,
    )
```

time: 136 us -> 115 us (0.85)
  local copies, waits for them, and re-layouts: 11 us -> 0 us
  Pallas kernels: 124 us -> 114 us
    unnamed x19 -> x0, local copies, waits for them, and re-layouts: 11 us -> none
    pallas_call x1 -> x2, Pallas kernels: 124 us -> 114 us  [the longest x1 111 us: per_device(): pl.pallas_call(body, out_shape=out_shape, in_specs=[smem, smem] + [anywhe...]
where the time goes in v2:
time: 115 us; the launch traced here: 114 us
  Pallas kernels  114 us (99%)
    pallas_call x1, Pallas kernels, per_device(): pl.pallas_call(body, out_shape=out_shape, in_specs=[smem, smem] + [anywhe...  111 us
    pallas_call x1, Pallas kernels, per_device(): pl.pallas_call(hand_out, out_shape=out_shape, in_specs=[anywhere] * 5, ou...  2.67 us

profile of v2, /device:TPU:1, one launch (start us, length us, event | category | flops | bytes accessed | tf_op | source)
XLA Modules:
  0.0 114.5 jit_solution(10927942954366540295)
XLA Ops:
  0.6 111.2 %step.1 = (f32[384,256]{1,0:T(8,128)}, f32[384,256]{1,0:T(8,128)}, f32[384,256]{1,0:T(8,128)}, bf16[3,128,2048]{2,1,0:T(8,128)(2,1)}, bf16[4,4,2048]{2,1,0:T(4,128)(2,1)}) custom-call(s32[4,2,4]{2,1,0:T(2,128)} %bitcast.15, f32[4,2,4]{2,1,0:T(2,128)} %bitcast.16, f32[384,256]{1,0:T(8,128)} %bitcast.10, f32[384,256]{1,0:T(8,128)} %bitcast.11, ...), custom_call_target="tpu_custom_call" | custom-call | tf_op jit(solution)/shard_map/step/pallas_call | solution.py:526
  111.8 2.7 %hand_out.1 = (f32[384,256]{1,0:T(8,128)}, f32[384,256]{1,0:T(8,128)}, f32[384,256]{1,0:T(8,128)}, bf16[3,128,2048]{2,1,0:T(8,128)(2,1)}, bf16[4,4,2048]{2,1,0:T(4,128)(2,1)}) custom-call(f32[384,256]{1,0:T(8,128)} %get-tuple-element.15.refs_0_, f32[384,256]{1,0:T(8,128)} %get-tuple-element.16.refs_1_, f32[384,256]{1,0:T(8,128)} %get-tuple-element.17.refs_2_, ...), custom_call_target="tpu_custom_call" | custom-call | tf_op jit(solution)/shard_map/hand_out/pallas_call | solution.py:594

commit v3 on v2

--- a/solution.py
+++ b/solution.py
@@ -100,6 +100,7 @@
     y_sem,
     core_sem,
     ret_sem,
+    turn_sem,
     back_sem,
     end_sem,
     wz_sem,
@@ -164,11 +165,11 @@
         load.start()
 
     meta_row = lax.broadcasted_iota(jnp.int32, (8, 128), 0)
-    meta_lane = lax.broadcasted_iota(jnp.int32, (8, 128), 1) - zh * 8
+    meta_lane = lax.broadcasted_iota(jnp.int32, (8, 128), 1) - zh * 16
     tile = jnp.zeros((8, 128), F32)
     for s in range(4):
         for r in range(4):
-            spot = meta_lane == 32 * (s // 2) + 4 * (s % 2) + r
+            spot = meta_lane == 4 * s + r
             for k in range(2):
                 tile = jnp.where(spot & (meta_row == k), ids_ref[s, k, r].astype(F32), tile)
                 tile = jnp.where(spot & (meta_row == 2 + k), gates_ref[s, k, r], tile)
@@ -180,8 +181,7 @@
     rows = wide[...]
     factor = lax.rsqrt(jnp.mean(rows * rows, axis=1, keepdims=True) + norm_eps)
     normed = rows * factor * gain_ref[...]
-    zrows[0, zh] = normed[0:8].astype(BF16)
-    zrows[1, zh] = normed[8:16].astype(BF16)
+    zrows[zh] = normed.astype(BF16)
     loads[2].wait()
     squares = jnp.zeros((8, 128), F32)
     for block in range(12):
@@ -213,7 +213,7 @@
                     send(meta.at[0], meta.at[j], meta_sem, (j - 1,), turn(ZH_AXIS, zh, j))
                 )
                 token_copies.append(
-                    send(zrows.at[:, zh], zrows.at[:, zh], tok_sem, (j - 1,), turn(ZH_AXIS, zh, j))
+                    send(zrows.at[zh], zrows.at[zh], tok_sem, (j - 1,), turn(ZH_AXIS, zh, j))
                 )
         if phase == 3:
             permute_z = one_hot_rows(lambda a, b, c, i: ((b * 4 + c) * 4 + a) * 2 + i)
@@ -287,7 +287,9 @@
     earlier = matmul(named.astype(BF16), before)
     slot_row = lax.broadcasted_iota(jnp.int32, (32, 64), 0)
     row_lane = lax.broadcasted_iota(jnp.int32, (32, 64), 1)
-    same_block = jnp.where(slot_row // 2 == row_lane // 4, 1.0, 0.0)
+    same_block = jnp.where(
+        (slot_row // 8 == (row_lane // 4) % 4) & ((slot_row // 2) % 4 == row_lane // 16), 1.0, 0.0
+    )
     slot_number = (slot_row % 2).astype(F32)
     hits = [jnp.where(earlier[p : p + 1, :] == slot_number, same_block, 0.0) for p in range(8)]
     token_rows = zrows[...].reshape(64, WIDTH)
@@ -305,33 +307,15 @@
                 stage.at[d - 1], slots.at[pl.ds(0, 2), d], x_sem, (d - 1,), turn(X_AXIS, x, d)
             )
     weights = []
-    for h in range(2):
-        columns = [hits[p] * share[p : p + 1, :] for p in range(8)]
-        columns = [c[16 * h : 16 * h + 16, 32 * h : 32 * h + 32] for c in columns]
+    for s in range(4):
+        columns = [(hits[p] * share[p : p + 1, :])[8 * s : 8 * s + 8] for p in range(8)]
         weight = jnp.concatenate(columns, axis=0).T
+        weight = jnp.concatenate([weight[16 * i + 4 * s : 16 * i + 4 * s + 4] for i in range(4)])
         high = weight.astype(BF16)
         rest = weight - high.astype(F32)
         middle = rest.astype(BF16)
         low = (rest - middle.astype(F32)).astype(BF16)
-        weights.append((high, middle, low))
-
-    y_copies = []
-    for k in range(3):
-        for copy in z_copies[3 * k : 3 * k + 3]:
-            copy.wait_recv()
-        gathered = wz_in[k].reshape(128, PART)
-        wy_out[k] = matmul(permute_y, gathered).astype(BF16).reshape(4, 32, PART)
-        for j in (2, 1, 3):
-            y_copies.append(
-                send(
-                    wy_out.at[k, (y + j) % 4],
-                    wy_in.at[k, y],
-                    wy_sem,
-                    (k, j - 1),
-                    turn(Y_AXIS, y, j),
-                )
-            )
-        wy_in[k, y] = wy_out[k, y]
+        weights.append(jnp.concatenate([high, middle, low], axis=0))
 
     over_y, over_core = {}, []
 
@@ -345,65 +329,111 @@
         over_y[d].wait_recv()
         over_core.append(send(slots.at[3, d], slots.at[4, d], core_sem, (1, d), next_core))
 
-    spread(0)
-
     def columns_of(position):
         return pl.ds(pl.multiple_of((2 * position + core) * PART, PART), PART)
 
     own_rows = pl.ds(pl.multiple_of(32 * x, 32), 32)
-    wx_copies = []
-    for k in range(3):
-        for copy in y_copies[3 * k : 3 * k + 3]:
+    across = {Y_AXIS: partner, C_AXIS: odd}
+    y_copies, wx_copies, core_copies, line_sends = {}, {}, {0: [], 1: [], 2: []}, []
+
+    def over_wy(k):
+        for copy in z_copies[3 * k : 3 * k + 3]:
+            copy.wait_recv()
+        gathered = wz_in[k].reshape(128, PART)
+        wy_out[k] = matmul(permute_y, gathered).astype(BF16).reshape(4, 32, PART)
+        y_copies[k] = [
+            send(wy_out.at[k, (y + j) % 4], wy_in.at[k, y], wy_sem, (k, j - 1), turn(Y_AXIS, y, j))
+            for j in (2, 1, 3)
+        ]
+        wy_in[k, y] = wy_out[k, y]
+
+    def over_wx(k):
+        for copy in y_copies[k]:
             copy.wait_recv()
         gathered = wy_in[k].reshape(128, PART)
         wx_out[k] = matmul(permute_x, gathered).astype(BF16).reshape(4, 32, PART)
-        for j in (2, 1, 3):
-            wx_copies.append(
-                send(
-                    wx_out.at[k, (x + j) % 4],
-                    wall.at[odd, k, own_rows, columns_of(zl)],
-                    wx_sem,
-                    (k, j - 1),
-                    turn(X_AXIS, x, j),
-                )
+        wx_copies[k] = [
+            send(
+                wx_out.at[k, (x + j) % 4],
+                wall.at[odd, k, own_rows, columns_of(zl)],
+                wx_sem,
+                (k, j - 1),
+                turn(X_AXIS, x, j),
             )
+            for j in (2, 1, 3)
+        ]
         wall[odd, k, own_rows, columns_of(zl)] = wx_out[k, x]
 
-    across = {Y_AXIS: partner, C_AXIS: odd}
-    line_copies = []
-    core_copies = []
+    def line_copy(k, position, number, arrival, target):
+        piece = wall.at[odd, k, :, columns_of(position)]
+        return pltpu.make_async_remote_copy(
+            src_ref=piece,
+            dst_ref=piece,
+            send_sem=wl_sem.at[0, k, number],
+            recv_sem=wl_sem.at[1, k, arrival],
+            device_id={ZL_AXIS: target},
+            device_id_type=MESH,
+        )
+
+    def line_send(copy, wanted):
+        @pl.when(wanted)
+        def _():
+            copy.start()
+
+        line_sends.append((copy, wanted))
 
     def share_out(k, j, position):
         piece = wall.at[odd, k, :, columns_of(position)]
         send(piece, piece, wp_sem, (k, 2 * j + core), across)
-        core_copies.append(send(piece, piece, wc_sem, (k, j), next_core))
-
-    for k in range(3):
-        for copy in wx_copies[3 * k : 3 * k + 3]:
+        core_copies[k].append(send(piece, piece, wc_sem, (k, j), next_core))
+
+    def over_line(k):
+        for copy in wx_copies[k]:
             copy.wait_recv()
-        mine = wall.at[odd, k, :, columns_of(zl)]
         for j in (2, 1, 3):
-            line_copies.append((k, j, send(mine, mine, wl_sem, (k, j - 1), turn(ZL_AXIS, zl, j))))
+            near = True if j == 2 else (zl != (3 if j == 1 else 0))
+            line_send(line_copy(k, zl, j - 1, j - 1, (zl + j) % 4), near)
         share_out(k, 0, zl)
+
+    late = jnp.where(zl == 0, 1, 3)
+    relay_to = jnp.where(zl == 2, 3, 0)
+
+    def onward(k):
+        for j in (2, 4 - late, late):
+            position = (zl + 4 - j) % 4
+            line_copy(k, position, j - 1, j - 1, zl).wait_recv()
+            if isinstance(j, int):
+                relayed = line_copy(k, position, 3, jnp.where(zl == 2, 2, 0), relay_to)
+                line_send(relayed, (zl == 1) | (zl == 2))
+            share_out(k, j, position)
+
+    over_wy(0)
+    over_wy(1)
+    over_wx(0)
+    over_wy(2)
+    over_wx(1)
+    over_line(0)
+    spread(0)
+    over_wx(2)
+    over_line(1)
     spread(1)
     forward(0)
+    over_line(2)
+    onward(0)
     spread(3)
     forward(1)
+    onward(1)
     spread(2)
-    for k, j, copy in line_copies:
-        copy.wait_recv()
-        share_out(k, j, (zl + 4 - j) % 4)
     forward(3)
+    onward(2)
     forward(2)
-    for copy in core_copies:
-        copy.wait_recv()
-    keep(wall.at[odd], served_hbm)
-    for copy in over_core:
-        copy.wait_recv()
-
-    @pl.when(core != odd)
-    def _():
-        for k in range(3):
+
+    def wait_weights(k):
+        for copy in core_copies[k]:
+            copy.wait_recv()
+
+        @pl.when(core != odd)
+        def _():
             for number in range(8):
                 piece = wall.at[core, k, :, pl.ds(PART * number, PART)]
                 pltpu.make_async_remote_copy(
@@ -415,75 +445,102 @@
                     device_id_type=MESH,
                 ).wait_recv()
 
+    for copy in over_core:
+        copy.wait_recv()
+    wait_weights(0)
+    wait_weights(1)
+
     into = wall.at[core, pl.ds(0, 2)]
-    swaps = []
+    active = []
     for h in range(2):
         taken = slots[pl.ds(1, 4), :, pl.ds(16 * h, 16), :].reshape(256, WIDTH)
         projected = matmul_nt(taken, into[...].reshape(256, WIDTH)) * (1.0 / math.sqrt(WIDTH))
         gate, up = projected[:, :128], projected[:, 128:]
-        active = (gate / (1.0 + jnp.exp(-gate)) * up).astype(BF16)
+        active.append((gate / (1.0 + jnp.exp(-gate)) * up).astype(BF16))
+    wait_weights(2)
+    keep(wall.at[odd], served_hbm)
+    swaps = []
+    for h in range(2):
         for i in range(4):
             span = pl.ds(512 * i, 512)
-            out = matmul(active, wall[core, 2, :, span]) * (1.0 / math.sqrt(HIDDEN))
-            answers[h, :, :, :, span] = out.astype(BF16).reshape(4, 4, 16, 512)
-        for number in (3, 1):
-            swaps.append(
-                send(
-                    answers.at[h, number],
-                    from_core.at[h, number // 2],
-                    ret_sem,
-                    (h, number // 2),
-                    next_core,
+            out = matmul(active[h], wall[core, 2, :, span]) * (1.0 / math.sqrt(HIDDEN))
+            out = out.reshape(4, 4, 16, 512)
+            answers[2 * h, :, :, :, span] = out[:, :, 0:8].astype(BF16)
+            answers[2 * h + 1, :, :, :, span] = out[:, :, 8:16].astype(BF16)
+        for s in (2 * h, 2 * h + 1):
+            for number in (3, 1):
+                swaps.append(
+                    send(
+                        answers.at[s, number],
+                        from_core.at[s, number // 2],
+                        ret_sem,
+                        (s, number // 2),
+                        next_core,
+                    )
                 )
+
+    over_y = []
+    for s in range(4):
+        swaps[2 * s].wait_recv()
+        relay[s] = (answers[s, 2].astype(F32) + from_core[s, 1].astype(F32)).astype(BF16)
+        over_y.append(send(relay.at[s], joined.at[s, 1], turn_sem, (s,), {Y_AXIS: other}))
+    for s in range(4):
+        swaps[2 * s + 1].wait_recv()
+        joined[s, 0] = (answers[s, 0].astype(F32) + from_core[s, 0].astype(F32)).astype(BF16)
+
+    over_x, over_z = {}, {}
+
+    def along_x(s):
+        over_y[s].wait_recv()
+        over_x[s] = [
+            send(joined.at[s, :, d], back.at[s, d], back_sem, (s, d), turn(X_AXIS, x, 4 - d))
+            for d in (2, 1, 3)
+        ]
+        back[s, 0] = joined[s, :, 0]
+
+    def to_rows(s):
+        for copy in over_x[s]:
+            copy.wait_recv()
+        made = matmul(weights[s], back[s].reshape(64, WIDTH))
+        made = made[0:16] + made[16:32] + made[32:48]
+        for i in range(4):
+            parts[s, i] = made[4 * i : 4 * i + 4].astype(BF16)
+        over_z[s] = [
+            send(
+                parts.at[s, (zh + j) % 4],
+                parts_in.at[s, j - 1],
+                end_sem,
+                (s, j - 1),
+                turn(ZH_AXIS, zh, j),
             )
-
-    over_y = []
-    for h in range(2):
-        swaps[2 * h].wait_recv()
-        relay[h] = (answers[h, 2].astype(F32) + from_core[h, 1].astype(F32)).astype(BF16)
-        over_y.append(send(relay.at[h], joined.at[h, 1], ret_sem, (h, 2), {Y_AXIS: other}))
-        swaps[2 * h + 1].wait_recv()
-        joined[h, 0] = (answers[h, 0].astype(F32) + from_core[h, 0].astype(F32)).astype(BF16)
-    over_x = []
-    for h in range(2):
-        over_y[h].wait_recv()
-        for d in (2, 1, 3):
-            over_x.append(
-                send(joined.at[h, :, d], back.at[h, d], back_sem, (h, d), turn(X_AXIS, x, 4 - d))
-            )
-        back[h, 0] = joined[h, :, 0]
-
-    over_z = []
-    for h in range(2):
-        for copy in over_x[3 * h : 3 * h + 3]:
-            copy.wait_recv()
-        held = back[h].reshape(128, WIDTH)
-        made = matmul(weights[h][0], held) + matmul(weights[h][1], held) + matmul(weights[h][2], held)
-        made = made.reshape(4, 8, WIDTH)
-        parts[h] = made.astype(BF16)
-        for j in (2, 1, 3):
-            over_z.append(
-                send(
-                    parts.at[h, (zh + j) % 4],
-                    parts_in.at[h, j - 1],
-                    end_sem,
-                    (h, j - 1),
-                    turn(ZH_AXIS, zh, j),
-                )
-            )
-    for h in range(2):
-        result = wide[pl.ds(8 * h, 8), :] + parts[h, zh].astype(F32)
-        for copy in over_z[3 * h : 3 * h + 3]:
+            for j in (2, 1, 3)
+        ]
+
+    along_x(0)
+    along_x(1)
+    to_rows(0)
+    along_x(2)
+    to_rows(1)
+    along_x(3)
+    to_rows(2)
+    to_rows(3)
+    for s in range(4):
+        result = wide[pl.ds(4 * s, 4), :] + parts[s, zh].astype(F32)
+        for copy in over_z[s]:
             copy.wait_recv()
         for j in range(3):
-            result = result + parts_in[h, j].astype(F32)
-        decoded_ref[2 * h] = result[0:4].astype(BF16)
-        decoded_ref[2 * h + 1] = result[4:8].astype(BF16)
+            result = result + parts_in[s, j].astype(F32)
+        decoded_ref[s] = result.astype(BF16)
     keep(decoded_ref, decoded_hbm)
     for copy in stores:
         copy.wait()
     for copy in started:
         copy.wait_send()
+    for copy, wanted in line_sends:
+
+        @pl.when(wanted)
+        def _(copy=copy):
+            copy.wait_send()
 
 
 def hand_out(*refs):
@@ -540,19 +597,19 @@
             pltpu.VMEM((1, WIDTH), F32),
             pltpu.VMEM((4, 4, WIDTH), BF16),
             pltpu.VMEM((16, WIDTH), F32),
-            pltpu.VMEM((2, 4, 8, WIDTH), BF16),
+            pltpu.VMEM((4, 16, WIDTH), BF16),
             pltpu.VMEM((4, 8, 128), F32),
             pltpu.VMEM((4, 8, 128), F32),
             pltpu.VMEM((22, 8, 128), F32),
             pltpu.VMEM((3, 2, BLOCK, WIDTH), BF16),
             pltpu.VMEM((5, 4, BLOCK, WIDTH), BF16),
-            pltpu.VMEM((2, 4, 4, 16, WIDTH), BF16),
-            pltpu.VMEM((2, 2, 4, 16, WIDTH), BF16),
-            pltpu.VMEM((2, 4, 16, WIDTH), BF16),
-            pltpu.VMEM((2, 2, 4, 16, WIDTH), BF16),
-            pltpu.VMEM((2, 4, 2, 16, WIDTH), BF16),
-            pltpu.VMEM((2, 4, 8, WIDTH), BF16),
-            pltpu.VMEM((2, 3, 8, WIDTH), BF16),
+            pltpu.VMEM((4, 4, 4, 8, WIDTH), BF16),
+            pltpu.VMEM((4, 2, 4, 8, WIDTH), BF16),
+            pltpu.VMEM((4, 4, 8, WIDTH), BF16),
+            pltpu.VMEM((4, 2, 4, 8, WIDTH), BF16),
+            pltpu.VMEM((4, 4, 2, 8, WIDTH), BF16),
+            pltpu.VMEM((4, 4, 4, WIDTH), BF16),
+            pltpu.VMEM((4, 3, 4, WIDTH), BF16),
             pltpu.VMEM((3, 4, 32, PART), BF16),
             pltpu.VMEM((3, 4, 32, PART), BF16),
             pltpu.VMEM((3, 4, 32, PART), BF16),
@@ -567,13 +624,14 @@
             dma((2, 3)),
             dma((2, 4)),
             dma((2, 2, 4)),
-            dma((2, 2, 3)),
-            dma((2, 2, 4)),
-            dma((2, 2, 3)),
+            dma((2, 4, 2)),
+            dma((2, 4)),
+            dma((2, 4, 4)),
+            dma((2, 4, 3)),
             dma((2, 3, 3)),
             dma((2, 3, 3)),
             dma((2, 3, 3)),
-            dma((2, 3, 3)),
+            dma((2, 3, 4)),
             dma((2, 3, 4)),
             dma((2, 3, 8)),
         ],

time: 115 us -> 110 us (0.957)
  Pallas kernels: 114 us -> 109 us
    pallas_call x1, Pallas kernels: 111 us -> 107 us  [per_device(): pl.pallas_call(body, out_shape=out_shape, in_specs=[smem, smem] + [anywhe...]
where the time goes in v3:
time: 110 us
  Pallas kernels  109 us (99%)
    pallas_call x1, Pallas kernels, per_device(): pl.pallas_call(body, out_shape=out_shape, in_specs=[smem, smem] + [anywhe...  107 us
    pallas_call x1, Pallas kernels, per_device(): pl.pallas_call(hand_out, out_shape=out_shape, in_specs=[anywhere] * 5, ou...  2.67 us

profile of v3, /device:TPU:1, one launch (start us, length us, event | category | flops | bytes accessed | tf_op | source)
XLA Modules:
  0.0 109.9 jit_solution(6318133517006392803)
XLA Ops:
  0.6 106.6 %step.1 = (f32[384,256]{1,0:T(8,128)}, f32[384,256]{1,0:T(8,128)}, f32[384,256]{1,0:T(8,128)}, bf16[3,128,2048]{2,1,0:T(8,128)(2,1)}, bf16[4,4,2048]{2,1,0:T(4,128)(2,1)}) custom-call(s32[4,2,4]{2,1,0:T(2,128)} %bitcast.15, f32[4,2,4]{2,1,0:T(2,128)} %bitcast.16, f32[384,256]{1,0:T(8,128)} %bitcast.10, f32[384,256]{1,0:T(8,128)} %bitcast.11, ...), custom_call_target="tpu_custom_call" | custom-call | tf_op jit(solution)/shard_map/step/pallas_call | solution.py:583
  107.3 2.7 %hand_out.1 = (f32[384,256]{1,0:T(8,128)}, f32[384,256]{1,0:T(8,128)}, f32[384,256]{1,0:T(8,128)}, bf16[3,128,2048]{2,1,0:T(8,128)(2,1)}, bf16[4,4,2048]{2,1,0:T(4,128)(2,1)}) custom-call(f32[384,256]{1,0:T(8,128)} %get-tuple-element.15.refs_0_, f32[384,256]{1,0:T(8,128)} %get-tuple-element.16.refs_1_, f32[384,256]{1,0:T(8,128)} %get-tuple-element.17.refs_2_, ...), custom_call_target="tpu_custom_call" | custom-call | tf_op jit(solution)/shard_map/hand_out/pallas_call | solution.py:652

commit v4 on v3

--- a/solution.py
+++ b/solution.py
@@ -91,6 +91,7 @@
     wy_in,
     wx_out,
     wall,
+    active,
     in_sem,
     out_sem,
     sum_sem,
@@ -173,7 +174,7 @@
             for k in range(2):
                 tile = jnp.where(spot & (meta_row == k), ids_ref[s, k, r].astype(F32), tile)
                 tile = jnp.where(spot & (meta_row == 2 + k), gates_ref[s, k, r], tile)
-    meta[0] = tile
+    meta[0] = tile[0:4]
     loads[0].wait()
     loads[1].wait()
     for s in range(4):
@@ -183,13 +184,17 @@
     normed = rows * factor * gain_ref[...]
     zrows[zh] = normed.astype(BF16)
     loads[2].wait()
-    squares = jnp.zeros((8, 128), F32)
-    for block in range(12):
-        values = grad_ref[pl.ds(32 * block, 32), :].astype(F32)
+
+    def add_block(block, squares):
+        values = grad_ref[pl.ds(pl.multiple_of(32 * block, 32), 32), :].astype(F32)
         values = values * values
         for i in range(4):
             for h in range(2):
                 squares = squares + values[8 * i : 8 * i + 8, 128 * h : 128 * h + 128]
+        return squares
+
+    squares = lax.fori_loop(0, 12, add_block, jnp.zeros((8, 128), F32))
+    squares = jnp.sum(squares, axis=0, keepdims=True)
     sums_out[0] = squares
     pl.semaphore_wait(barrier, len(peers))
 
@@ -230,6 +235,50 @@
     total = jnp.sum(squares, axis=(0, 1), keepdims=True)
     clip = jnp.minimum(1.0, lax.rsqrt(total * (1.0 / COUNT) + norm_eps))
 
+    x_copies = {}
+    hits = []
+    routed = []
+
+    def pick():
+        for copy in token_copies:
+            copy.wait_recv()
+        routes = meta[0] + meta[1] + meta[2] + meta[3]
+        id_one, id_two = routes[0:1, 0:64], routes[1:2, 0:64]
+        gate_one, gate_two = routes[2:3, 0:64], routes[3:4, 0:64]
+        gate_sum = gate_one + gate_two
+        share_one, share_two = gate_one / gate_sum, gate_two / gate_sum
+        place = lax.broadcasted_iota(jnp.int32, (8, 64), 0)
+        expert = (2 * ((x + place // 2) % 4) + (pair + place % 2) % 2).astype(F32)
+        names_one = jnp.where(id_one == expert, 1.0, 0.0)
+        names_two = jnp.where(id_two == expert, 1.0, 0.0)
+        named = names_one + names_two
+        share = names_one * share_one + names_two * share_two
+        above = lax.broadcasted_iota(jnp.int32, (64, 64), 0)
+        below = lax.broadcasted_iota(jnp.int32, (64, 64), 1)
+        before = jnp.where((above // 4 == below // 4) & (above < below), 1.0, 0.0).astype(BF16)
+        earlier = matmul(named.astype(BF16), before)
+        slot_row = lax.broadcasted_iota(jnp.int32, (32, 64), 0)
+        row_lane = lax.broadcasted_iota(jnp.int32, (32, 64), 1)
+        same_block = jnp.where(
+            (slot_row // 8 == (row_lane // 4) % 4) & ((slot_row // 2) % 4 == row_lane // 16), 1.0, 0.0
+        )
+        slot_number = (slot_row % 2).astype(F32)
+        hits[:] = [jnp.where(earlier[p : p + 1, :] == slot_number, same_block, 0.0) for p in range(8)]
+        token_rows = zrows[...].reshape(64, WIDTH)
+        for d in (0, 2, 1, 3):
+            picks = [hits[2 * d + r] * named[2 * d + r : 2 * d + r + 1, :] for r in (1, 0)]
+            chosen = matmul(jnp.concatenate(picks, axis=0).astype(BF16), token_rows)
+            chosen = chosen.astype(BF16).reshape(2, BLOCK, WIDTH)
+            if d == 0:
+                slots[0, 0] = chosen[0]
+                slots[1, 0] = chosen[1]
+            else:
+                stage[d - 1] = chosen
+                x_copies[d] = send(
+                    stage.at[d - 1], slots.at[pl.ds(0, 2), d], x_sem, (d - 1,), turn(X_AXIS, x, d)
+                )
+        routed.append(share)
+
     first_fix = 1.0 / (1.0 - beta_one**step_count)
     second_fix = 1.0 / (1.0 - beta_two**step_count)
     z_copies = []
@@ -241,8 +290,9 @@
         stores.append(copy)
 
     for k in range(3):
-        for block in range(4):
-            at = pl.ds(128 * k + 32 * block, 32)
+        @pl.loop(0, 4)
+        def _(block, k=k):
+            at = pl.ds(pl.multiple_of(128 * k + 32 * block, 32), 32)
             scaled = grad_ref[at, :].astype(F32) * clip
             first = beta_one * one_ref[at, :] + (1.0 - beta_one) * scaled
             second = beta_two * two_ref[at, :] + (1.0 - beta_two) * scaled * scaled
@@ -251,6 +301,7 @@
             new_master_ref[at, :] = old - learn_rate * (update + decay_rate * old)
             new_one_ref[at, :] = first
             new_two_ref[at, :] = second
+
         rounded = new_master_ref[pl.ds(128 * k, 128), :].astype(BF16)
         wz_out[k] = matmul(permute_z, rounded).astype(BF16).reshape(4, 32, PART)
         for j in (2, 1, 3):
@@ -264,58 +315,11 @@
                 )
             )
         wz_in[k, zh] = wz_out[k, zh]
+        if k == 0:
+            pick()
     keep(new_master_ref, new_master_hbm)
     keep(new_one_ref, new_one_hbm)
     keep(new_two_ref, new_two_hbm)
-
-    for copy in token_copies:
-        copy.wait_recv()
-    routes = meta[0] + meta[1] + meta[2] + meta[3]
-    id_one, id_two = routes[0:1, 0:64], routes[1:2, 0:64]
-    gate_one, gate_two = routes[2:3, 0:64], routes[3:4, 0:64]
-    gate_sum = gate_one + gate_two
-    share_one, share_two = gate_one / gate_sum, gate_two / gate_sum
-    place = lax.broadcasted_iota(jnp.int32, (8, 64), 0)
-    expert = (2 * ((x + place // 2) % 4) + (pair + place % 2) % 2).astype(F32)
-    names_one = jnp.where(id_one == expert, 1.0, 0.0)
-    names_two = jnp.where(id_two == expert, 1.0, 0.0)
-    named = names_one + names_two
-    share = names_one * share_one + names_two * share_two
-    above = lax.broadcasted_iota(jnp.int32, (64, 64), 0)
-    below = lax.broadcasted_iota(jnp.int32, (64, 64), 1)
-    before = jnp.where((above // 4 == below // 4) & (above < below), 1.0, 0.0).astype(BF16)
-    earlier = matmul(named.astype(BF16), before)
-    slot_row = lax.broadcasted_iota(jnp.int32, (32, 64), 0)
-    row_lane = lax.broadcasted_iota(jnp.int32, (32, 64), 1)
-    same_block = jnp.where(
-        (slot_row // 8 == (row_lane // 4) % 4) & ((slot_row // 2) % 4 == row_lane // 16), 1.0, 0.0
-    )
-    slot_number = (slot_row % 2).astype(F32)
-    hits = [jnp.where(earlier[p : p + 1, :] == slot_number, same_block, 0.0) for p in range(8)]
-    token_rows = zrows[...].reshape(64, WIDTH)
-    x_copies = {}
-    for d in (0, 2, 1, 3):
-        picks = [hits[2 * d + r] * named[2 * d + r : 2 * d + r + 1, :] for r in (1, 0)]
-        chosen = matmul(jnp.concatenate(picks, axis=0).astype(BF16), token_rows)
-        chosen = chosen.astype(BF16).reshape(2, BLOCK, WIDTH)
-        if d == 0:
-            slots[0, 0] = chosen[0]
-            slots[1, 0] = chosen[1]
-        else:
-            stage[d - 1] = chosen
-            x_copies[d] = send(
-                stage.at[d - 1], slots.at[pl.ds(0, 2), d], x_sem, (d - 1,), turn(X_AXIS, x, d)
-            )
-    weights = []
-    for s in range(4):
-        columns = [(hits[p] * share[p : p + 1, :])[8 * s : 8 * s + 8] for p in range(8)]
-        weight = jnp.concatenate(columns, axis=0).T
-        weight = jnp.concatenate([weight[16 * i + 4 * s : 16 * i + 4 * s + 4] for i in range(4)])
-        high = weight.astype(BF16)
-        rest = weight - high.astype(F32)
-        middle = rest.astype(BF16)
-        low = (rest - middle.astype(F32)).astype(BF16)
-        weights.append(jnp.concatenate([high, middle, low], axis=0))
 
     over_y, over_core = {}, []
 
@@ -420,6 +424,17 @@
     forward(0)
     over_line(2)
     onward(0)
+    weights = []
+    for s in range(4):
+        columns = [(hits[p] * routed[0][p : p + 1, :])[8 * s : 8 * s + 8] for p in range(8)]
+        weight = jnp.concatenate(columns, axis=0).T
+        weight = jnp.concatenate([weight[16 * i + 4 * s : 16 * i + 4 * s + 4] for i in range(4)])
+        high = weight.astype(BF16)
+        rest = weight - high.astype(F32)
+        middle = rest.astype(BF16)
+        low = (rest - middle.astype(F32)).astype(BF16)
+        weights.append(jnp.concatenate([high, middle, low], axis=0))
+
     spread(3)
     forward(1)
     onward(1)
@@ -451,22 +466,27 @@
     wait_weights(1)
 
     into = wall.at[core, pl.ds(0, 2)]
-    active = []
-    for h in range(2):
-        taken = slots[pl.ds(1, 4), :, pl.ds(16 * h, 16), :].reshape(256, WIDTH)
-        projected = matmul_nt(taken, into[...].reshape(256, WIDTH)) * (1.0 / math.sqrt(WIDTH))
+
+    @pl.loop(0, 2)
+    def _(h):
+        taken = slots[pl.ds(1, 4), :, pl.ds(pl.multiple_of(16 * h, 16), 16), :]
+        projected = matmul_nt(taken.reshape(256, WIDTH), into[...].reshape(256, WIDTH))
+        projected = projected * (1.0 / math.sqrt(WIDTH))
         gate, up = projected[:, :128], projected[:, 128:]
-        active.append((gate / (1.0 + jnp.exp(-gate)) * up).astype(BF16))
+        active[h] = (gate / (1.0 + jnp.exp(-gate)) * up).astype(BF16)
+
     wait_weights(2)
     keep(wall.at[odd], served_hbm)
     swaps = []
     for h in range(2):
-        for i in range(4):
-            span = pl.ds(512 * i, 512)
+        @pl.loop(0, 4)
+        def _(i, h=h):
+            span = pl.ds(pl.multiple_of(512 * i, 512), 512)
             out = matmul(active[h], wall[core, 2, :, span]) * (1.0 / math.sqrt(HIDDEN))
             out = out.reshape(4, 4, 16, 512)
             answers[2 * h, :, :, :, span] = out[:, :, 0:8].astype(BF16)
             answers[2 * h + 1, :, :, :, span] = out[:, :, 8:16].astype(BF16)
+
         for s in (2 * h, 2 * h + 1):
             for number in (3, 1):
                 swaps.append(
@@ -598,9 +618,9 @@
             pltpu.VMEM((4, 4, WIDTH), BF16),
             pltpu.VMEM((16, WIDTH), F32),
             pltpu.VMEM((4, 16, WIDTH), BF16),
-            pltpu.VMEM((4, 8, 128), F32),
-            pltpu.VMEM((4, 8, 128), F32),
-            pltpu.VMEM((22, 8, 128), F32),
+            pltpu.VMEM((4, 4, 128), F32),
+            pltpu.VMEM((4, 1, 128), F32),
+            pltpu.VMEM((22, 1, 128), F32),
             pltpu.VMEM((3, 2, BLOCK, WIDTH), BF16),
             pltpu.VMEM((5, 4, BLOCK, WIDTH), BF16),
             pltpu.VMEM((4, 4, 4, 8, WIDTH), BF16),
@@ -616,6 +636,7 @@
             pltpu.VMEM((3, 4, 32, PART), BF16),
             pltpu.VMEM((3, 4, 32, PART), BF16),
             pltpu.VMEM((2, 3, 128, WIDTH), BF16),
+            pltpu.VMEM((2, 256, 128), BF16),
             dma((6,)),
             dma((5,)),
             dma((2, 22)),

time: 110 us -> 109 us (level); the launches traced: 110 us -> 108 us
  Pallas kernels: 109 us -> 107 us
    pallas_call x1, Pallas kernels: 107 us -> 104 us  [per_device(): pl.pallas_call(body, out_shape=out_shape, in_specs=[smem, smem] + [anywhe...]
where the time goes in v4:
time: 109 us; the launch traced here: 108 us
  Pallas kernels  107 us (98%)
    pallas_call x1, Pallas kernels, per_device(): pl.pallas_call(body, out_shape=out_shape, in_specs=[smem, smem] + [anywhe...  104 us
    pallas_call x1, Pallas kernels, per_device(): pl.pallas_call(hand_out, out_shape=out_shape, in_specs=[anywhere] * 5, ou...  2.67 us

profile of v4, /device:TPU:1, one launch (start us, length us, event | category | flops | bytes accessed | tf_op | source)
XLA Modules:
  0.0 107.8 jit_solution(11479124888606737252)
XLA Ops:
  0.6 104.5 %step.1 = (f32[384,256]{1,0:T(8,128)}, f32[384,256]{1,0:T(8,128)}, f32[384,256]{1,0:T(8,128)}, bf16[3,128,2048]{2,1,0:T(8,128)(2,1)}, bf16[4,4,2048]{2,1,0:T(4,128)(2,1)}) custom-call(s32[4,2,4]{2,1,0:T(2,128)} %bitcast.15, f32[4,2,4]{2,1,0:T(2,128)} %bitcast.16, f32[384,256]{1,0:T(8,128)} %bitcast.10, f32[384,256]{1,0:T(8,128)} %bitcast.11, ...), custom_call_target="tpu_custom_call" | custom-call | tf_op jit(solution)/shard_map/step/pallas_call | solution.py:603
  105.1 2.7 %hand_out.1 = (f32[384,256]{1,0:T(8,128)}, f32[384,256]{1,0:T(8,128)}, f32[384,256]{1,0:T(8,128)}, bf16[3,128,2048]{2,1,0:T(8,128)(2,1)}, bf16[4,4,2048]{2,1,0:T(4,128)(2,1)}) custom-call(f32[384,256]{1,0:T(8,128)} %get-tuple-element.15.refs_0_, f32[384,256]{1,0:T(8,128)} %get-tuple-element.16.refs_1_, f32[384,256]{1,0:T(8,128)} %get-tuple-element.17.refs_2_, ...), custom_call_target="tpu_custom_call" | custom-call | tf_op jit(solution)/shard_map/hand_out/pallas_call | solution.py:673

commit v5 on v4

--- a/solution.py
+++ b/solution.py
@@ -145,7 +145,13 @@
 
     barrier = pltpu.get_barrier_semaphore()
     peers = [along_z(j) for j in (8, 7, 9, 6, 10, 5, 11, 4, 12, 3, 13, 2, 14, 1, 15)]
-    peers += [turn(axis, me, j) for axis, me in ((X_AXIS, x), (Y_AXIS, y)) for j in (2, 1, 3)]
+    plane = [
+        {X_AXIS: (x + i) % 4, Y_AXIS: (y + j) % 4}
+        for i in (2, 1, 3, 0)
+        for j in (2, 1, 3, 0)
+        if i or j
+    ]
+    peers += plane
     peers += [{Y_AXIS: partner, C_AXIS: 1 - core}, next_core]
     for peer in peers:
         pl.semaphore_signal(barrier, inc=1, device_id=peer, device_id_type=MESH)
@@ -203,8 +209,7 @@
     for phase, devices in enumerate(
         (
             [along_z(j) for j in (8, 7, 9, 6, 10, 5, 11, 4, 12, 3, 13, 2, 14, 1, 15)],
-            [turn(X_AXIS, x, j) for j in (2, 1, 3)],
-            [turn(Y_AXIS, y, j) for j in (2, 1, 3)],
+            plane,
             [next_core],
         )
     ):
@@ -220,7 +225,7 @@
                 token_copies.append(
                     send(zrows.at[zh], zrows.at[zh], tok_sem, (j - 1,), turn(ZH_AXIS, zh, j))
                 )
-        if phase == 3:
+        if phase == 2:
             permute_z = one_hot_rows(lambda a, b, c, i: ((b * 4 + c) * 4 + a) * 2 + i)
             permute_y = one_hot_rows(lambda a, b, c, i: ((c * 4 + b) * 4 + a) * 2 + i)
             permute_x = one_hot_rows(lambda a, b, c, i: ((b * 4 + a) * 4 + c) * 2 + i)
@@ -230,7 +235,7 @@
             copy.wait_recv()
             squares = squares + sums_in[slot + i]
         slot += len(copies)
-        if phase < 3:
+        if phase < 2:
             sums_out[phase + 1] = squares
     total = jnp.sum(squares, axis=(0, 1), keepdims=True)
     clip = jnp.minimum(1.0, lax.rsqrt(total * (1.0 / COUNT) + norm_eps))
@@ -619,8 +624,8 @@
             pltpu.VMEM((16, WIDTH), F32),
             pltpu.VMEM((4, 16, WIDTH), BF16),
             pltpu.VMEM((4, 4, 128), F32),
-            pltpu.VMEM((4, 1, 128), F32),
-            pltpu.VMEM((22, 1, 128), F32),
+            pltpu.VMEM((3, 1, 128), F32),
+            pltpu.VMEM((31, 1, 128), F32),
             pltpu.VMEM((3, 2, BLOCK, WIDTH), BF16),
             pltpu.VMEM((5, 4, BLOCK, WIDTH), BF16),
             pltpu.VMEM((4, 4, 4, 8, WIDTH), BF16),
@@ -639,7 +644,7 @@
             pltpu.VMEM((2, 256, 128), BF16),
             dma((6,)),
             dma((5,)),
-            dma((2, 22)),
+            dma((2, 31)),
             dma((2, 3)),
             dma((2, 3)),
             dma((2, 3)),

time: 109 us -> 109 us (level)
  no operation moved by 1% of the time
where the time goes in v5:
time: 109 us; the launch traced here: 107 us
  Pallas kernels  107 us (98%)
    pallas_call x1, Pallas kernels, per_device(): pl.pallas_call(body, out_shape=out_shape, in_specs=[smem, smem] + [anywhe...  104 us
    pallas_call x1, Pallas kernels, per_device(): pl.pallas_call(hand_out, out_shape=out_shape, in_specs=[anywhere] * 5, ou...  2.67 us

profile of v5, /device:TPU:1, one launch (start us, length us, event | category | flops | bytes accessed | tf_op | source)
XLA Modules:
  0.0 107.5 jit_solution(17280106426465445984)
XLA Ops:
  0.6 104.2 %step.1 = (f32[384,256]{1,0:T(8,128)}, f32[384,256]{1,0:T(8,128)}, f32[384,256]{1,0:T(8,128)}, bf16[3,128,2048]{2,1,0:T(8,128)(2,1)}, bf16[4,4,2048]{2,1,0:T(4,128)(2,1)}) custom-call(s32[4,2,4]{2,1,0:T(2,128)} %bitcast.15, f32[4,2,4]{2,1,0:T(2,128)} %bitcast.16, f32[384,256]{1,0:T(8,128)} %bitcast.10, f32[384,256]{1,0:T(8,128)} %bitcast.11, ...), custom_call_target="tpu_custom_call" | custom-call | tf_op jit(solution)/shard_map/step/pallas_call | solution.py:608
  104.8 2.7 %hand_out.1 = (f32[384,256]{1,0:T(8,128)}, f32[384,256]{1,0:T(8,128)}, f32[384,256]{1,0:T(8,128)}, bf16[3,128,2048]{2,1,0:T(8,128)(2,1)}, bf16[4,4,2048]{2,1,0:T(4,128)(2,1)}) custom-call(f32[384,256]{1,0:T(8,128)} %get-tuple-element.15.refs_0_, f32[384,256]{1,0:T(8,128)} %get-tuple-element.16.refs_1_, f32[384,256]{1,0:T(8,128)} %get-tuple-element.17.refs_2_, ...), custom_call_target="tpu_custom_call" | custom-call | tf_op jit(solution)/shard_map/hand_out/pallas_call | solution.py:678
